TPU v7x, 32 devices: a whole 2x2x4 slice. The times are simulated.
32 devices in a mesh: dp: 2 (over core), tensor: 16 (over z, y, x).
Axes of the slice: x: 2, y: 2, z: 4, core: 2. Of those that a mesh axis runs over, the one named last changes fastest.
Arguments:
- sequence_entries: float32 [8192, 1024], P(('dp', 'tensor')), may hold values from -6 to 6
- running_dividend: float32 [4, 1024], P('dp', 'tensor'), may hold values from -6 to 6
- running_divisor: float32 [4, 1024], P('dp', 'tensor'), may hold values from 1 to 4
- running_exponent: float32 [4, 1024], P('dp', 'tensor'), may hold values from -1 to 2
- preceding_attend: bfloat16 [4, 1024], P('dp'), may hold values from -6 to 6
- preceding_feedforward: bfloat16 [4, 1024], P('dp'), may hold values from -6 to 6
- first_norm_factor: float32 [1024], replicated, may hold values from 0.5 to 1.5
- first_norm_shift: float32 [1024], replicated, may hold values from -3 to 3
- attend_fading: float32 [1024], replicated, may hold values from -6.2 to -2.3
- instant_reward: float32 [1024], replicated, may hold values from -1 to 1
- attend_kshare: float32 [1024], replicated, may hold values from 0.05 to 0.95
- attend_vshare: float32 [1024], replicated, may hold values from 0.05 to 0.95
- attend_rshare: float32 [1024], replicated, may hold values from 0.05 to 0.95
- attend_kmatrix: bfloat16 [1024, 1024], P('dp', 'tensor'), may hold values from -0.1875 to 0.1875
- attend_vmatrix: bfloat16 [1024, 1024], P('dp', 'tensor'), may hold values from -0.1875 to 0.1875
- attend_rmatrix: bfloat16 [1024, 1024], P('dp', 'tensor'), may hold values from -0.1875 to 0.1875
- attend_omatrix: bfloat16 [1024, 1024], P('dp', 'tensor'), may hold values from -0.75 to 0.75
- second_norm_factor: float32 [1024], replicated, may hold values from 0.5 to 1.5
- second_norm_shift: float32 [1024], replicated, may hold values from -3 to 3
- feedforward_kshare: float32 [1024], replicated, may hold values from 0.05 to 0.95
- feedforward_rshare: float32 [1024], replicated, may hold values from 0.05 to 0.95
- feedforward_kmatrix: bfloat16 [1024, 4096], P('dp', 'tensor'), may hold values from -0.1875 to 0.1875
- feedforward_vmatrix: bfloat16 [1024, 4096], P('dp', 'tensor'), may hold values from -0.09375 to 0.09375
- feedforward_rmatrix: bfloat16 [1024, 1024], P('dp', 'tensor'), may hold values from -0.1875 to 0.1875
- upstream_gradient: float32 [8192, 1024], P(('dp', 'tensor')), may hold values from -6 to 6
Outputs:
- block_out: float32 [8192, 1024], P(('dp', 'tensor'))
- tokens_grad: float32 [8192, 1024], P(('dp', 'tensor'))
- state_num_grad: float32 [4, 1024], P('dp', 'tensor')
- state_den_grad: float32 [4, 1024], P('dp', 'tensor')
- state_top_grad: float32 [4, 1024], P('dp', 'tensor')
- prev_time_grad: float32 [4, 1024], P('dp')
- prev_channel_grad: float32 [4, 1024], P('dp')
- norm1_gain_grad: float32 [1024], replicated
- norm1_bias_grad: float32 [1024], replicated
- time_decay_grad: float32 [1024], replicated
- time_first_grad: float32 [1024], replicated
- time_mix_key_grad: float32 [1024], replicated
- time_mix_value_grad: float32 [1024], replicated
- time_mix_recept_grad: float32 [1024], replicated
- key_weight_grad: float32 [1024, 1024], P('dp', 'tensor')
- value_weight_grad: float32 [1024, 1024], P('dp', 'tensor')
- recept_weight_grad: float32 [1024, 1024], P('dp', 'tensor')
- out_weight_grad: float32 [1024, 1024], P('dp', 'tensor')
- norm2_gain_grad: float32 [1024], replicated
- norm2_bias_grad: float32 [1024], replicated
- chan_mix_key_grad: float32 [1024], replicated
- chan_mix_recept_grad: float32 [1024], replicated
- chan_key_weight_grad: float32 [1024, 4096], P('dp', 'tensor')
- chan_value_weight_grad: float32 [1024, 4096], P('dp', 'tensor')
- chan_recept_weight_grad: float32 [1024, 1024], P('dp', 'tensor')
All inputs are finite; a program needn't handle non-finite values.
Results may differ from a plain program's by a relative error of at most 0.02.
Values may be sent and summed in bfloat16 or wider, within the bound.
A program may use at most 384 MiB of HBM per device.

v0:
```python
import jax
import jax.numpy as jnp
from jax import lax
from jax.sharding import PartitionSpec as P

SEGMENT = 2048
SPAN_LENGTH = 64


epsilon = 1e-05


def layer_norm(vals_matrix, gain, offset):
    center = vals_matrix - jnp.mean(vals_matrix, axis=-1, keepdims=True)
    spread = jnp.mean(center * center, axis=-1, keepdims=True)
    return center * lax.rsqrt(spread + epsilon) * gain + offset


def span_blend(running_bundle, pieces):
    running_dividend, running_divisor, running_exponent, fading_rates, reward_terms = running_bundle
    span_keys_matrix, span_values = pieces
    length = span_keys_matrix.shape[0]
    places = jnp.arange(length)
    offsets = places.astype(span_keys_matrix.dtype)
    distance = offsets[:, None] - 1.0 - offsets[None, :]
    earlier = span_keys_matrix[None, :, :] - distance[:, :, None] * fading_rates[None, None, :]
    instant_entry = reward_terms[None, :] + span_keys_matrix
    before_mask = (places[None, :] < places[:, None])[:, :, None]
    same_mask = (places[None, :] == places[:, None])[:, :, None]
    scores = jnp.where(before_mask, earlier, jnp.where(same_mask, instant_entry[None, :, :], -1e30))
    carried = running_exponent[None, :] - offsets[:, None] * fading_rates[None, :]
    highest = jnp.maximum(jnp.max(scores, axis=1), carried)
    weights = jnp.exp(scores - highest[:, None, :])
    kept_weight = jnp.exp(carried - highest)
    numerator = (
        jnp.sum(weights * span_values[None, :, :], axis=1) + kept_weight * running_dividend[None, :]
    )
    denominator = jnp.sum(weights, axis=1) + kept_weight * running_divisor[None, :]
    result_matrix = numerator / denominator
    tail_scores = span_keys_matrix - (length - 1.0 - offsets)[:, None] * fading_rates[None, :]
    old_score = running_exponent - length * fading_rates
    updated_exponent = jnp.maximum(jnp.max(tail_scores, axis=0), old_score)
    tail_weight = jnp.exp(tail_scores - updated_exponent[None, :])
    old_weight = jnp.exp(old_score - updated_exponent)
    updated_dividend = jnp.sum(tail_weight * span_values, axis=0) + old_weight * running_dividend
    updated_divisor = jnp.sum(tail_weight, axis=0) + old_weight * running_divisor
    return (
        (updated_dividend, updated_divisor, updated_exponent, fading_rates, reward_terms),
        result_matrix,
    )


def recurrent_average(
    whole_keys_matrix,
    whole_vals_matrix,
    fading_rates,
    reward_terms,
    running_dividend,
    running_divisor,
    running_exponent,
):
    length, feature_count = whole_keys_matrix.shape
    span_sequence = length // SPAN_LENGTH
    final_recurrent, result_matrix = lax.scan(
        jax.checkpoint(span_blend),
        (running_dividend, running_divisor, running_exponent, fading_rates, reward_terms),
        (
            whole_keys_matrix.reshape(span_sequence, SPAN_LENGTH, feature_count),
            whole_vals_matrix.reshape(span_sequence, SPAN_LENGTH, feature_count),
        ),
    )
    return result_matrix.reshape(length, feature_count)


def recept_core(
    keys_matrix,
    vals_matrix,
    recept_pre,
    decay_part,
    prefix_slice,
    running_dividend,
    running_divisor,
    running_exponent,
):
    cluster_sequence, feature_indices = running_dividend.shape

    def to_time(array):
        return jnp.transpose(
            array.reshape(cluster_sequence, SEGMENT, feature_indices), (1, 0, 2)
        ).reshape(SEGMENT, cluster_sequence * feature_indices)

    fading_rates = jnp.tile(jnp.exp(decay_part), cluster_sequence)
    reward_terms = jnp.tile(prefix_slice, cluster_sequence)
    blended_source = recurrent_average(
        to_time(keys_matrix),
        to_time(vals_matrix),
        fading_rates,
        reward_terms,
        running_dividend.reshape(-1),
        running_divisor.reshape(-1),
        running_exponent.reshape(-1),
    )
    blended_source = jnp.transpose(
        blended_source.reshape(SEGMENT, cluster_sequence, feature_indices), (1, 0, 2)
    ).reshape(cluster_sequence * SEGMENT, feature_indices)
    return jax.nn.sigmoid(recept_pre) * blended_source


def earlier_rows(gathered, previous):
    cluster_sequence = previous.shape[0]
    shaped = gathered.reshape(cluster_sequence, SEGMENT, gathered.shape[1])
    joined = jnp.concatenate([previous[:, None, :], shaped[:, :-1, :]], axis=1)
    return joined.reshape(gathered.shape)


def blended(instant_entry, before, mixing):
    return (
        instant_entry.astype(jnp.float32) * mixing + before.astype(jnp.float32) * (1.0 - mixing)
    ).astype(jnp.bfloat16)


def pushed_back(back_part, cluster_sequence):
    shaped = back_part.reshape(cluster_sequence, SEGMENT, back_part.shape[1])
    moved = jnp.concatenate([shaped[:, 1:, :], jnp.zeros_like(shaped[:, :1, :])], axis=1)
    return (moved.reshape(back_part.shape), shaped[:, 0, :])


def contract_rows(left, right):
    return lax.dot_general(
        left, right, (((0,), (0,)), ((), ())), preferred_element_type=jnp.float32
    )


def contract_cols(left, right):
    return lax.dot_general(
        left, right, (((1,), (1,)), ((), ())), preferred_element_type=jnp.float32
    )


def local(
    sequence_entries,
    running_dividend,
    running_divisor,
    running_exponent,
    preceding_attend,
    preceding_feedforward,
    first_norm_factor,
    first_norm_shift,
    attend_fading,
    instant_reward,
    attend_kshare,
    attend_vshare,
    attend_rshare,
    attend_kmatrix,
    attend_vmatrix,
    attend_rmatrix,
    attend_omatrix,
    second_norm_factor,
    second_norm_shift,
    feedforward_kshare,
    feedforward_rshare,
    feedforward_kmatrix,
    feedforward_vmatrix,
    feedforward_rmatrix,
    upstream_gradient,
):
    own_rows = sequence_entries.shape[0]
    tensor_place = lax.axis_index("tensor")
    row_start = tensor_place * own_rows
    cluster_sequence = preceding_attend.shape[0]
    feature_indices = running_dividend.shape[1]
    feature_count = sequence_entries.shape[1]
    initial_feature = tensor_place * feature_indices
    decay_part = lax.dynamic_slice_in_dim(attend_fading, initial_feature, feature_indices)
    prefix_slice = lax.dynamic_slice_in_dim(instant_reward, initial_feature, feature_indices)

    def fetch_weights():
        shards = (
            lax.all_gather(attend_kmatrix, "dp", axis=0, tiled=True),
            lax.all_gather(attend_vmatrix, "dp", axis=0, tiled=True),
            lax.all_gather(attend_rmatrix, "dp", axis=0, tiled=True),
            lax.all_gather(attend_omatrix, "dp", axis=0, tiled=True),
            lax.all_gather(feedforward_kmatrix, "dp", axis=0, tiled=True),
            lax.all_gather(feedforward_vmatrix, "dp", axis=0, tiled=True),
            lax.all_gather(feedforward_rmatrix, "dp", axis=0, tiled=True),
        )
        whole_recept = lax.all_gather(shards[6], "tensor", axis=1, tiled=True)
        whole_out = shards[3]
        return (shards, whole_recept, whole_out)

    def gather_first(normed):
        return lax.all_gather(normed, "tensor", axis=0, tiled=True)

    def gather_second(normed):
        return lax.all_gather(normed, "tensor", axis=0, tiled=True)

    shards, whole_recept, whole_out = fetch_weights()
    key_local, value_local, recept_local, out_local, chan_key_local, chan_value_local = shards[:6]
    normed_first = layer_norm(sequence_entries, first_norm_factor, first_norm_shift).astype(
        jnp.bfloat16
    )
    gathered_first = gather_first(normed_first)
    before_first = earlier_rows(gathered_first, preceding_attend)
    key_in = blended(gathered_first, before_first, attend_kshare)
    value_in = blended(gathered_first, before_first, attend_vshare)
    recept_in = blended(gathered_first, before_first, attend_rshare)
    keys_matrix = jnp.dot(key_in, key_local, preferred_element_type=jnp.float32)
    vals_matrix = jnp.dot(value_in, value_local, preferred_element_type=jnp.float32)
    recept_pre = jnp.dot(recept_in, recept_local, preferred_element_type=jnp.float32)
    gated_output, core_pull = jax.vjp(
        recept_core,
        keys_matrix,
        vals_matrix,
        recept_pre,
        decay_part,
        prefix_slice,
        running_dividend,
        running_divisor,
        running_exponent,
    )
    gated_low = gated_output.astype(jnp.bfloat16)
    attn_rows = lax.psum_scatter(
        contract_cols(gated_low, out_local), "tensor", scatter_dimension=0, tiled=True
    )
    middle = sequence_entries + attn_rows
    normed_second = layer_norm(middle, second_norm_factor, second_norm_shift).astype(jnp.bfloat16)
    gathered_second = gather_second(normed_second)
    before_second = earlier_rows(gathered_second, preceding_feedforward)
    chan_key_in = blended(gathered_second, before_second, feedforward_kshare)
    own_before = lax.dynamic_slice_in_dim(before_second, row_start, own_rows, 0)
    chan_rec_in = blended(normed_second, own_before, feedforward_rshare)
    hidden = jnp.dot(chan_key_in, chan_key_local, preferred_element_type=jnp.float32)
    squared = jnp.square(jax.nn.relu(hidden)).astype(jnp.bfloat16)
    chan_values = lax.psum_scatter(
        contract_cols(squared, chan_value_local), "tensor", scatter_dimension=0, tiled=True
    )
    chan_gate = jax.nn.sigmoid(
        jnp.dot(chan_rec_in, whole_recept, preferred_element_type=jnp.float32)
    )
    result = middle + chan_gate * chan_values
    shards, whole_recept, whole_out = fetch_weights()
    key_local, value_local, recept_local, out_local, chan_key_local, chan_value_local = shards[:6]
    grad_values_rows = (upstream_gradient * chan_gate).astype(jnp.bfloat16)
    grad_gate_pre = (upstream_gradient * chan_values * chan_gate * (1.0 - chan_gate)).astype(
        jnp.bfloat16
    )
    grad_chan_recept = contract_rows(chan_rec_in, grad_gate_pre)
    grad_rec_in = contract_cols(grad_gate_pre, whole_recept)
    grad_values_all = lax.all_gather(grad_values_rows, "tensor", axis=0, tiled=True)
    grad_squared = jnp.dot(grad_values_all, chan_value_local, preferred_element_type=jnp.float32)
    grad_chan_value = contract_rows(grad_values_all, squared)
    grad_hidden = (grad_squared * 2.0 * jax.nn.relu(hidden)).astype(jnp.bfloat16)
    gathered_second = gather_second(normed_second)
    before_second = earlier_rows(gathered_second, preceding_feedforward)
    chan_key_in = blended(gathered_second, before_second, feedforward_kshare)
    grad_chan_key = contract_rows(chan_key_in, grad_hidden)
    grad_key_in = contract_cols(grad_hidden, chan_key_local)
    second_diff = gathered_second.astype(jnp.float32) - before_second.astype(jnp.float32)
    grad_mix_ck = jnp.sum(grad_key_in * second_diff, axis=0)
    own_diff = normed_second.astype(jnp.float32) - own_before.astype(jnp.float32)
    grad_mix_cr = jnp.sum(grad_rec_in * own_diff, axis=0)
    own_grad = grad_key_in * feedforward_kshare
    back_grad = grad_key_in * (1.0 - feedforward_kshare)
    own_grad = lax.dynamic_update_slice_in_dim(
        own_grad,
        lax.dynamic_slice_in_dim(own_grad, row_start, own_rows, 0)
        + grad_rec_in * feedforward_rshare,
        row_start,
        0,
    )
    back_grad = lax.dynamic_update_slice_in_dim(
        back_grad,
        lax.dynamic_slice_in_dim(back_grad, row_start, own_rows, 0)
        + grad_rec_in * (1.0 - feedforward_rshare),
        row_start,
        0,
    )
    moved_second, grad_prev_channel = pushed_back(back_grad, cluster_sequence)
    grad_second_rows = lax.psum_scatter(
        own_grad + moved_second, "tensor", scatter_dimension=0, tiled=True
    )
    unused_second, pull_second = jax.vjp(layer_norm, middle, second_norm_factor, second_norm_shift)
    grad_mid_norm, grad_gain_two, grad_bias_two = pull_second(grad_second_rows)
    grad_middle = upstream_gradient + grad_mid_norm
    grad_attn_rows = grad_middle.astype(jnp.bfloat16)
    grad_attn_all = lax.all_gather(grad_attn_rows, "tensor", axis=0, tiled=True)
    grad_gated = jnp.dot(grad_attn_all, out_local, preferred_element_type=jnp.float32)
    grad_out_whole = contract_rows(grad_attn_all, gated_low)
    (
        grad_keys,
        grad_vals,
        grad_recept,
        grad_decay_part,
        grad_first_part,
        grad_num,
        grad_den,
        grad_top,
    ) = core_pull(grad_gated)
    grad_keys = grad_keys.astype(jnp.bfloat16)
    grad_vals = grad_vals.astype(jnp.bfloat16)
    grad_recept = grad_recept.astype(jnp.bfloat16)
    gathered_first = gather_first(normed_first)
    before_first = earlier_rows(gathered_first, preceding_attend)
    key_in = blended(gathered_first, before_first, attend_kshare)
    value_in = blended(gathered_first, before_first, attend_vshare)
    recept_in = blended(gathered_first, before_first, attend_rshare)
    grad_key_weight = contract_rows(key_in, grad_keys)
    grad_value_weight = contract_rows(value_in, grad_vals)
    grad_recept_weight = contract_rows(recept_in, grad_recept)
    first_diff = gathered_first.astype(jnp.float32) - before_first.astype(jnp.float32)
    input_key = contract_cols(grad_keys, key_local)
    grad_mix_tk = jnp.sum(input_key * first_diff, axis=0)
    own_first = input_key * attend_kshare
    back_first = input_key * (1.0 - attend_kshare)
    input_value = contract_cols(grad_vals, value_local)
    grad_mix_tv = jnp.sum(input_value * first_diff, axis=0)
    own_first = own_first + input_value * attend_vshare
    back_first = back_first + input_value * (1.0 - attend_vshare)
    input_recept = contract_cols(grad_recept, recept_local)
    grad_mix_tr = jnp.sum(input_recept * first_diff, axis=0)
    own_first = own_first + input_recept * attend_rshare
    back_first = back_first + input_recept * (1.0 - attend_rshare)
    moved_first, grad_prev_time = pushed_back(back_first, cluster_sequence)
    grad_first_rows = lax.psum_scatter(
        (own_first + moved_first).astype(jnp.bfloat16), "tensor", scatter_dimension=0, tiled=True
    ).astype(jnp.float32)
    unused_first, pull_first = jax.vjp(
        layer_norm, sequence_entries, first_norm_factor, first_norm_shift
    )
    grad_tok_norm, grad_gain_one, grad_bias_one = pull_first(grad_first_rows)
    tokens_grad = grad_middle + grad_tok_norm
    recept_cols_grad = lax.psum_scatter(
        grad_chan_recept.astype(jnp.bfloat16), "tensor", scatter_dimension=1, tiled=True
    )
    weight_sums = (
        lax.psum_scatter(
            grad_key_weight.astype(jnp.bfloat16), "dp", scatter_dimension=0, tiled=True
        ).astype(jnp.float32),
        lax.psum_scatter(
            grad_value_weight.astype(jnp.bfloat16), "dp", scatter_dimension=0, tiled=True
        ).astype(jnp.float32),
        lax.psum_scatter(
            grad_recept_weight.astype(jnp.bfloat16), "dp", scatter_dimension=0, tiled=True
        ).astype(jnp.float32),
        lax.psum_scatter(
            grad_out_whole.astype(jnp.bfloat16), "dp", scatter_dimension=0, tiled=True
        ).astype(jnp.float32),
        lax.psum_scatter(
            grad_chan_key.astype(jnp.bfloat16), "dp", scatter_dimension=0, tiled=True
        ).astype(jnp.float32),
        lax.psum_scatter(
            grad_chan_value.astype(jnp.bfloat16), "dp", scatter_dimension=0, tiled=True
        ).astype(jnp.float32),
        lax.psum_scatter(recept_cols_grad, "dp", scatter_dimension=0, tiled=True).astype(
            jnp.float32
        ),
    )
    decay_full = lax.dynamic_update_slice_in_dim(
        jnp.zeros((feature_count,), jnp.float32), grad_decay_part, initial_feature, 0
    )
    first_full = lax.dynamic_update_slice_in_dim(
        jnp.zeros((feature_count,), jnp.float32), grad_first_part, initial_feature, 0
    )
    vector_stack = jnp.stack(
        [
            grad_gain_one,
            grad_bias_one,
            decay_full,
            first_full,
            grad_mix_tk,
            grad_mix_tv,
            grad_mix_tr,
            grad_gain_two,
            grad_bias_two,
            grad_mix_ck,
            grad_mix_cr,
        ]
    )
    dp_count = lax.axis_size("dp")
    dp_place = lax.axis_index("dp")
    previous_pair = jnp.stack([grad_prev_time, grad_prev_channel])[:, None, :, :]
    previous_all = lax.dynamic_update_slice(
        jnp.zeros((2, dp_count, cluster_sequence, feature_count), jnp.float32),
        previous_pair,
        (0, dp_place, 0, 0),
    )
    vector_sums, previous_sums = lax.psum((vector_stack, previous_all), ("dp", "tensor"))
    previous_mine = lax.dynamic_index_in_dim(previous_sums, dp_place, axis=1, keepdims=False)
    return (
        result,
        tokens_grad,
        grad_num,
        grad_den,
        grad_top,
        previous_mine[0],
        previous_mine[1],
        vector_sums[0],
        vector_sums[1],
        vector_sums[2],
        vector_sums[3],
        vector_sums[4],
        vector_sums[5],
        vector_sums[6],
        weight_sums[0],
        weight_sums[1],
        weight_sums[2],
        weight_sums[3],
        vector_sums[7],
        vector_sums[8],
        vector_sums[9],
        vector_sums[10],
        weight_sums[4],
        weight_sums[5],
        weight_sums[6],
    )


def solution(mesh):
    return jax.shard_map(
        local,
        mesh=mesh,
        in_specs=(
            P(("dp", "tensor"), None),
            P("dp", "tensor"),
            P("dp", "tensor"),
            P("dp", "tensor"),
            P("dp", None),
            P("dp", None),
            P(),
            P(),
            P(),
            P(),
            P(),
            P(),
            P(),
            P("dp", "tensor"),
            P("dp", "tensor"),
            P("dp", "tensor"),
            P("dp", "tensor"),
            P(),
            P(),
            P(),
            P(),
            P("dp", "tensor"),
            P("dp", "tensor"),
            P("dp", "tensor"),
            P(("dp", "tensor"), None),
        ),
        out_specs=(
            P(("dp", "tensor"), None),
            P(("dp", "tensor"), None),
            P("dp", "tensor"),
            P("dp", "tensor"),
            P("dp", "tensor"),
            P("dp", None),
            P("dp", None),
            P(),
            P(),
            P(),
            P(),
            P(),
            P(),
            P(),
            P("dp", "tensor"),
            P("dp", "tensor"),
            P("dp", "tensor"),
            P("dp", "tensor"),
            P(),
            P(),
            P(),
            P(),
            P("dp", "tensor"),
            P("dp", "tensor"),
            P("dp", "tensor"),
        ),
        check_vma=False,
    )
```

profile of v0, /device:TPU:0, one launch (start us, length us, event | category | flops | bytes accessed | tf_op | source)
XLA Modules:
  0.0 3417.9 jit_solution(7833403810725060617)
XLA Ops:
  31.4 97.8 %all-gather.6.cloned.1.call-done = bf16[4096,1024]{1,0:T(8,128)(2,1)} async-done(((bf16[256,1024]{1,0:T(8,128)(2,1)}), bf16[4096,1024]{1,0:T(8,128)(2,1)}) %all-gather.6.cloned.1.call-update) | async-done | bytes 8388624 | tf_op jit(solution)/shard_map/all_gather | solution.py:192
  129.2 9.3 pad_maximum_fusion
  138.6 15.5 fusion.58
  163.2 6.0 fusion.99
  171.4 630.2 %while.60 = (s32[]{:T(128)}, f32[128]{0:T(128)S(1)}, f32[128]{0:T(128)}, f32[128]{0:T(128)S(1)}, f32[32,64,128]{2,1,0:T(8,128)}, /*index=5*/f32[32,128]{1,0:T(8,...) while((s32[]{:T(128)}, f32[128]{0:T(128)S(1)}, ...), condition=%wide.region_9.10_spmd.clone.clone.clone.clone, body=%wide.region_2.9_spmd.clone.clone.clone.sunk.clone | while | flops 6976578 | bytes 814289 | solution.py:64
  184.3 4.3 multiply_reduce_fusion.27
  204.0 4.3 multiply_reduce_fusion.27
  223.6 4.3 multiply_reduce_fusion.27
  243.3 4.3 multiply_reduce_fusion.27
  263.0 4.3 multiply_reduce_fusion.27
  282.7 4.3 multiply_reduce_fusion.27
  440.1 4.3 multiply_reduce_fusion.27
  577.9 4.3 multiply_reduce_fusion.27
  807.3 7.1 multiply_convert_fusion.3
  815.2 8.1 fusion.101
  823.4 344.7 %reduce-scatter.13.cloned.1.call-done = f32[256,1024]{1,0:T(8,128)} async-done(((f32[4096,1024]{1,0:T(8,128)}), f32[256,1024]{1,0:T(8,128)}) %reduce-scatter.13.cloned.1.call-update) | async-done | bytes 1048592 | tf_op jit(solution)/shard_map/reduce_scatter | solution.py:222
  1177.4 112.5 %all-gather.8.cloned.1.call-done = bf16[4096,1024]{1,0:T(8,128)(2,1)} async-done(((bf16[256,1024]{1,0:T(8,128)(2,1)}), bf16[4096,1024]{1,0:T(8,128)(2,1)}) %all-gather.8.cloned.1.call-update) | async-done | bytes 8388624 | tf_op jit(solution)/shard_map/all_gather | solution.py:195
  1289.9 9.3 pad_maximum_fusion.1
  1299.2 7.9 convolution_maximum_fusion
  1309.1 8.1 fusion.80
  1317.9 33.6 all-gather.10.cloned.1.call-done
  1351.5 347.2 %reduce-scatter.15.cloned.1.call-done = f32[256,1024]{1,0:T(8,128)} async-done(((f32[4096,1024]{1,0:T(8,128)}), f32[256,1024]{1,0:T(8,128)}) %reduce-scatter.15.cloned.1.call-update) | async-done | bytes 1048592 | tf_op jit(solution)/shard_map/reduce_scatter | solution.py:234
  1698.7 4.4 multiply_convert_fusion.1
  1703.1 118.6 %all-gather.12.cloned.1.call-done = bf16[4096,1024]{1,0:T(8,128)(2,1)} async-done(((bf16[256,1024]{1,0:T(8,128)(2,1)}), bf16[4096,1024]{1,0:T(8,128)(2,1)}) %all-gather.12.cloned.1.call-update) | async-done | bytes 8388624 | tf_op jit(solution)/shard_map/all_gather | solution.py:249
  1821.7 8.4 fusion.61
  1830.1 18.0 fusion.52
  1848.1 5.1 fusion.76
  1853.2 13.0 slice.82
  1866.2 14.2 concatenate.16
  1880.4 12.4 bitcast_add_fusion.3
  1896.2 341.4 %reduce-scatter.17.cloned.1.call-done = f32[256,1024]{1,0:T(8,128)} async-done(((f32[4096,1024]{1,0:T(8,128)}), f32[256,1024]{1,0:T(8,128)}) %reduce-scatter.17.cloned.1.call-update) | async-done | bytes 1048592 | tf_op jit(solution)/shard_map/reduce_scatter | solution.py:279
  2244.8 81.3 %reduce-scatter.33.cloned.1.call-done = bf16[1024,64]{0,1:T(8,128)(2,1)} async-done(((bf16[1024,1024]{0,1:T(8,128)(2,1)}), bf16[1024,64]{0,1:T(8,128)(2,1)}) %reduce-scatter.33.cloned.1.call-update) | async-done | bytes 131088 | tf_op jit(solution)/shard_map/reduce_scatter | solution.py:332
  2326.2 7.8 convolution_convert_fusion.1
  2334.2 12.5 convolution_convert_fusion.2
  2346.7 92.1 %all-gather.14.cloned.1.call-done = bf16[4096,1024]{1,0:T(8,128)(2,1)} async-done(((bf16[256,1024]{1,0:T(8,128)(2,1)}), bf16[4096,1024]{1,0:T(8,128)(2,1)}) %all-gather.14.cloned.1.call-update) | async-done | bytes 8388624 | tf_op jit(solution)/shard_map/all_gather | solution.py:286
  2438.8 7.1 fusion.96
  2451.3 528.3 %while.59 = (s32[]{:T(128)}, f32[128]{0:T(128)S(1)}, f32[128]{0:T(128)S(1)}, f32[128]{0:T(128)S(1)}, f32[128]{0:T(128)S(1)}, /*index=5*/f32[128]{0:T(128)S(1)}, ...) while((s32[]{:T(128)}, f32[128]{0:T(128)S(1)}, ...), condition=%wide.region_36.37_spmd.clone.clone, body=%wide.region_17.36_spmd.clone.sunk.clone | while | flops 24724292 | bytes 3444187 | solution.py:64
  2988.6 8.1 fusion.102
  2998.9 8.1 fusion.103
  3007.1 5.6 convolution_convert_fusion.4
  3012.8 5.6 convolution_convert_fusion.5
  3018.6 27.9 multiply_reduce_fusion.9
  3046.5 5.6 convolution_convert_fusion.6
  3052.1 11.8 slice.83
  3064.0 12.9 concatenate.17
  3076.9 25.4 fusion.59
  3118.0 160.8 %reduce-scatter.19.cloned.1.call-done = bf16[256,1024]{1,0:T(8,128)(2,1)} async-done(((bf16[4096,1024]{1,0:T(8,128)(2,1)}), bf16[256,1024]{1,0:T(8,128)(2,1)}) %reduce-scatter.19.cloned.1.call-update) | async-done | bytes 524304 | tf_op jit(solution)/shard_map/reduce_scatter | solution.py:324
  3285.7 122.1 %all-reduce.5.cloned.1.call-done = (f32[2,2,2,1024]{3,2,1,0:T(2,128)}, f32[11,1024]{1,0:T(8,128)}) async-done(((f32[2,2,2,1024]{3,2,1,0:T(2,128)}, f32[11,1024]{1,0:T(8,128)}), (f32[2,2,2,1024]{3,2,1,0:T(2,128)}, f32[11,1024]{1,0:T(8,128)})) %all-reduce.5.cloned.1.call-update) | async-done | bytes 77840 | tf_op jit(solution)/shard_map/psum | solution.py:387
  (2141 shorter events, 1226.7 us)
Async XLA Ops:
  7.2 122.0 %all-gather.6.cloned.1.call-start = ((), (), s32[]{:S(2)}) async-start(), calls=%async_computation.12 | async-start | bytes 8912896 | tf_op jit(solution)/shard_map/all_gather | solution.py:192
  13.6 1154.5 %reduce-scatter.13.cloned.1.call-start = ((), (), s32[]{:S(2)}) async-start(), calls=%async_computation.13 | async-start | bytes 17825792 | tf_op jit(solution)/shard_map/reduce_scatter | solution.py:222
  23.1 131.0 %copy-start.16 = (bf16[1024,64]{0,1:T(8,128)(2,1)}, bf16[1024,64]{0,1:T(8,128)(2,1)S(1)}, u32[]{:S(2)}) copy-start(bf16[1024,64]{0,1:T(8,128)(2,1)S(1)} %all_gather.49) | copy-start | bytes 393220
  25.4 780.9 %copy-start.18 = (bf16[1024,64]{0,1:T(8,128)(2,1)}, bf16[1024,64]{0,1:T(8,128)(2,1)S(1)}, u32[]{:S(2)}) copy-start(bf16[1024,64]{0,1:T(8,128)(2,1)S(1)} %all_gather.47) | copy-start | bytes 393220
  30.7 107.8 %copy-start.31 = (f32[1024]{0:T(1024)}, f32[1024]{0:T(1024)S(1)}, u32[]{:S(2)}) copy-start(f32[1024]{0:T(1024)S(1)} %broadcast_subtract_fusion.6) | copy-start | bytes 12292
  31.4 107.1 %copy-start.37 = (f32[1024]{0:T(1024)}, f32[1024]{0:T(1024)S(1)}, u32[]{:S(2)}) copy-start(f32[1024]{0:T(1024)S(1)} %get-tuple-element.1003) | copy-start | bytes 12292
  31.4 107.1 %copy-start.39 = (f32[1024]{0:T(1024)}, f32[1024]{0:T(1024)S(1)}, u32[]{:S(2)}) copy-start(f32[1024]{0:T(1024)S(1)} %get-tuple-element.1004) | copy-start | bytes 12292
  823.3 344.8 %copy-start.1 = (f32[256,1024]{1,0:T(8,128)S(1)}, f32[256,1024]{1,0:T(8,128)}, u32[]{:S(2)}) copy-start(f32[256,1024]{1,0:T(8,128)} %param.29) | copy-start | bytes 3145732
  823.3 346.5 %copy-start.25 = (f32[1024]{0:T(1024)S(1)}, f32[1024]{0:T(1024)}, u32[]{:S(2)}) copy-start(f32[1024]{0:T(1024)} %param.46) | copy-start | bytes 12292
  823.3 346.5 %copy-start.48 = (f32[1024]{0:T(1024)S(1)}, f32[1024]{0:T(1024)}, u32[]{:S(2)}) copy-start(f32[1024]{0:T(1024)} %param.47) | copy-start | bytes 12292
  823.3 347.6 %copy-start.23 = (bf16[512,64]{0,1:T(8,128)(2,1)S(1)}, bf16[512,64]{0,1:T(8,128)(2,1)}, u32[]{:S(2)}) copy-start(bf16[512,64]{0,1:T(8,128)(2,1)} %param.52) | copy-start | bytes 196612
  823.3 349.8 %copy-start.49 = (bf16[2,1024]{1,0:T(2,128)(2,1)S(1)}, bf16[2,1024]{1,0:T(2,128)(2,1)}, u32[]{:S(2)}) copy-start(bf16[2,1024]{1,0:T(2,128)(2,1)} %param.34) | copy-start | bytes 12292
  823.3 349.8 %copy-start.20 = (bf16[512,256]{1,0:T(8,128)(2,1)S(1)}, bf16[512,256]{1,0:T(8,128)(2,1)}, u32[]{:S(2)}) copy-start(bf16[512,256]{1,0:T(8,128)(2,1)} %param.50) | copy-start | bytes 786436
  823.3 351.9 %copy-start.21 = (bf16[512,256]{1,0:T(8,128)(2,1)S(1)}, bf16[512,256]{1,0:T(8,128)(2,1)}, u32[]{:S(2)}) copy-start(bf16[512,256]{1,0:T(8,128)(2,1)} %param.51) | copy-start | bytes 786436
  823.3 354.1 %copy-start.43 = (f32[1024]{0:T(1024)S(1)}, f32[1024]{0:T(1024)}, u32[]{:S(2)}) copy-start(f32[1024]{0:T(1024)} %param.48) | copy-start | bytes 12292
  823.3 466.6 %all-gather.8.cloned.1.call-start = ((), (), s32[]{:S(2)}) async-start(), calls=%async_computation.14 | async-start | bytes 8912896 | tf_op jit(solution)/shard_map/all_gather | solution.py:195
  1170.8 180.6 %all-gather.10.cloned.1.call-start = ((), (), s32[]{:S(2)}) async-start(), calls=%async_computation.15 | async-start | bytes 2228224 | tf_op jit(solution)/shard_map/all_gather | solution.py:187
  1173.0 525.7 %reduce-scatter.15.cloned.1.call-start = ((), (), s32[]{:S(2)}) async-start(), calls=%async_computation.16 | async-start | bytes 17825792 | tf_op jit(solution)/shard_map/reduce_scatter | solution.py:234
  1177.4 129.7 %copy-start.14 = (bf16[1024,256]{1,0:T(8,128)(2,1)}, bf16[1024,256]{1,0:T(8,128)(2,1)S(1)}, u32[]{:S(2)}) copy-start(bf16[1024,256]{1,0:T(8,128)(2,1)S(1)} %all_gather.55) | copy-start | bytes 1572868
  1317.2 381.5 %copy-start.4 = (bf16[256,1024]{1,0:T(8,128)(2,1)S(1)}, bf16[256,1024]{1,0:T(8,128)(2,1)}, u32[]{:S(2)}) copy-start(bf16[256,1024]{1,0:T(8,128)(2,1)} %add_convert_fusion) | copy-start | bytes 1572868
  1317.2 381.5 %copy-start.11 = (f32[256,1024]{1,0:T(8,128)S(1)}, f32[256,1024]{1,0:T(8,128)}, u32[]{:S(2)}) copy-start(f32[256,1024]{1,0:T(8,128)} %param.53) | copy-start | bytes 3145732
  1317.2 504.5 %all-gather.12.cloned.1.call-start = ((), (), s32[]{:S(2)}) async-start(), calls=%async_computation.17 | async-start | bytes 8912896 | tf_op jit(solution)/shard_map/all_gather | solution.py:249
  1703.1 534.5 %reduce-scatter.17.cloned.1.call-start = ((), (), s32[]{:S(2)}) async-start(), calls=%async_computation.18 | async-start | bytes 17825792 | tf_op jit(solution)/shard_map/reduce_scatter | solution.py:279
  1830.1 18.0 copy-start.15
  1853.2 27.2 slice-start.2
  1853.2 27.2 slice-start.3
  1866.2 14.2 slice-start.5
  1892.9 433.2 %reduce-scatter.33.cloned.1.call-start = ((), (), s32[]{:S(2)}) async-start(), calls=%async_computation.27 | async-start | bytes 2228224 | tf_op jit(solution)/shard_map/reduce_scatter | solution.py:332
  1896.1 542.7 %all-gather.14.cloned.1.call-start = ((), (), s32[]{:S(2)}) async-start(), calls=%async_computation.19 | async-start | bytes 8912896 | tf_op jit(solution)/shard_map/all_gather | solution.py:286
  2243.0 859.4 %reduce-scatter.35.cloned.1.call-start = ((), (), s32[]{:S(2)}) async-start(), calls=%async_computation.28 | async-start | bytes 196608 | tf_op jit(solution)/shard_map/reduce_scatter | solution.py:354
  2326.1 778.8 %reduce-scatter.31.cloned.1.call-start = ((), (), s32[]{:S(2)}) async-start(), calls=%async_computation.26 | async-start | bytes 786432 | tf_op jit(solution)/shard_map/reduce_scatter | solution.py:351
  2334.0 104.9 %copy-start.10 = (f32[2,8,8,2048]{3,2,0,1:T(8,128)S(1)}, f32[2,8,8,2048]{3,2,0,1:T(8,128)}, u32[]{:S(2)}) copy-start(f32[2,8,8,2048]{3,2,0,1:T(8,128)} %copy-done.9) | copy-start | bytes 3145732
  2334.0 772.8 %reduce-scatter.29.cloned.1.call-start = ((), (), s32[]{:S(2)}) async-start(), calls=%async_computation.25 | async-start | bytes 786432 | tf_op jit(solution)/shard_map/reduce_scatter | solution.py:348
  2346.7 765.3 %reduce-scatter.27.cloned.1.call-start = ((), (), s32[]{:S(2)}) async-start(), calls=%async_computation.24 | async-start | bytes 196608 | tf_op jit(solution)/shard_map/reduce_scatter | solution.py:345
  3007.0 106.5 %reduce-scatter.25.cloned.1.call-start = ((), (), s32[]{:S(2)}) async-start(), calls=%async_computation.23 | async-start | bytes 196608 | tf_op jit(solution)/shard_map/reduce_scatter | solution.py:342
  3012.8 102.3 %reduce-scatter.23.cloned.1.call-start = ((), (), s32[]{:S(2)}) async-start(), calls=%async_computation.22 | async-start | bytes 196608 | tf_op jit(solution)/shard_map/reduce_scatter | solution.py:339
  3018.5 98.1 %reduce-scatter.21.cloned.1.call-start = ((), (), s32[]{:S(2)}) async-start(), calls=%async_computation.21 | async-start | bytes 196608 | tf_op jit(solution)/shard_map/reduce_scatter | solution.py:336
  3063.9 214.9 %reduce-scatter.19.cloned.1.call-start = ((), (), s32[]{:S(2)}) async-start(), calls=%async_computation.20 | async-start | bytes 8912896 | tf_op jit(solution)/shard_map/reduce_scatter | solution.py:324
  3102.3 176.6 %copy-start.2 = (f32[256,1024]{1,0:T(8,128)S(1)}, f32[256,1024]{1,0:T(8,128)}, u32[]{:S(2)}) copy-start(f32[256,1024]{1,0:T(8,128)} %param.29) | copy-start | bytes 3145732
  3102.3 176.6 %copy-start.24 = (f32[1024]{0:T(1024)S(1)}, f32[1024]{0:T(1024)}, u32[]{:S(2)}) copy-start(f32[1024]{0:T(1024)} %param.35) | copy-start | bytes 12292
  3102.3 176.5 %copy-start.28 = (f32[256]{0:T(256)S(1)}, f32[256]{0:T(256)}, u32[]{:S(2)}) copy-start(f32[256]{0:T(256)} %copy-done.27) | copy-start | bytes 3076
  3102.3 178.0 %copy-start.47 = (f32[256]{0:T(256)S(1)}, f32[256]{0:T(256)}, u32[]{:S(2)}) copy-start(f32[256]{0:T(256)} %copy-done.46) | copy-start | bytes 3076
  3102.3 178.0 %copy-start.45 = (f32[256]{0:T(256)S(1)}, f32[256]{0:T(256)}, u32[]{:S(2)}) copy-start(f32[256]{0:T(256)} %copy-done.44) | copy-start | bytes 3076
  3102.3 179.6 %copy-start.41 = (f32[1024]{0:T(1024)S(1)}, f32[1024]{0:T(1024)}, u32[]{:S(2)}) copy-start(f32[1024]{0:T(1024)} %get-tuple-element.971) | copy-start | bytes 12292
  3102.3 179.6 %copy-start.42 = (f32[1024]{0:T(1024)S(1)}, f32[1024]{0:T(1024)}, u32[]{:S(2)}) copy-start(f32[1024]{0:T(1024)} %get-tuple-element.982) | copy-start | bytes 12292
  3102.4 180.9 %copy-start.12 = (f32[256,1024]{1,0:T(8,128)S(1)}, f32[256,1024]{1,0:T(8,128)}, u32[]{:S(2)}) copy-start(f32[256,1024]{1,0:T(8,128)} %param.53) | copy-start | bytes 3145732
  3102.4 305.4 %all-reduce.5.cloned.1.call-start = ((), (), s32[]{:S(2)}) async-start(), calls=%async_computation.29 | async-start | bytes 196608 | tf_op jit(solution)/shard_map/psum | solution.py:387
  3112.0 171.2 %copy-start.22 = (f32[2,2,2,1024]{3,2,1,0:T(2,128)}, f32[2,2,2,1024]{3,2,1,0:T(2,128)S(1)}, u32[]{:S(2)}) copy-start(f32[2,2,2,1024]{3,2,1,0:T(2,128)S(1)} %fusion.82) | copy-start | bytes 98308
  (27 other events, 162.2 us)
Sparse Core Ops, SparseCore 0:
  13.7 115.5 all-gather.5
  823.5 344.5 reduce-scatter.12
  1171.4 118.4 all-gather.7
  1292.5 58.8 all-gather.9
  1353.6 345.0 reduce-scatter.14
  1703.2 118.4 all-gather.11
  1893.0 344.5 reduce-scatter.16
  2239.8 86.2 reduce-scatter.32
  2328.9 109.9 all-gather.13
  2440.9 5.7 reduce-scatter.34
  2448.9 9.0 reduce-scatter.30
  2460.2 9.1 reduce-scatter.28
  3007.1 5.7 reduce-scatter.26
  3015.6 8.6 reduce-scatter.24
  3026.9 8.6 reduce-scatter.22
  3064.0 5.9 reduce-scatter.20
  3102.5 176.2 reduce-scatter.18
  3284.3 123.4 all-reduce.4
where the time goes:
time: 3450 us; the launch traced here: 3420 us
  waiting for transfers between devices  1850 us (54%)
  other arithmetic  819 us (24%)
  local copies, waits for them, and re-layouts  541 us (16%)
  matrix products  169 us (5%)
    reduce_scatter x1, waiting for transfers between devices, local(): lax.psum_scatter(contract_cols(squared, chan_value_local), 'tensor', scat...  347 us
    reduce_scatter x1, waiting for transfers between devices, local(): lax.psum_scatter(contract_cols(gated_low, out_local), 'tensor', scatter_d...  345 us
    reduce_scatter x1, waiting for transfers between devices, local(): lax.psum_scatter(own_grad + moved_second, 'tensor', scatter_dimension=0,...  341 us
    reduce_sum x64, other arithmetic, span_blend(): jnp.sum(weights * span_values[None, :, :], axis=1)  212 us
    dynamic_update_slice x160, local copies, waits for them, and re-layouts, recurrent_average(): lax.scan(jax.checkpoint(span_blend), (running_dividend, running_divisor,...  205 us
    squeeze x256, local copies, waits for them, and re-layouts, recurrent_average(): lax.scan(jax.checkpoint(span_blend), (running_dividend, running_divisor,...  183 us
    reduce_max x64, other arithmetic, span_blend(): highest = jnp.maximum(jnp.max(scores, axis=1), carried)  172 us
    reduce_scatter x1, waiting for transfers between devices, local(): lax.psum_scatter((own_first + moved_first).astype(jnp.bfloat16), 'tensor'...  161 us
  transfers between devices with their start and end apart: 18, of which 11 were waited for; matrix products, arithmetic and copies ran while one was open for 22% of the time, Pallas kernels for 0%

commit v1 on v0

v1 whole, which is shorter than its diff:
```python
import functools

import jax
import jax.numpy as jnp
from jax import lax
from jax.experimental import pallas as pl
from jax.experimental.pallas import tpu as pltpu
from jax.sharding import PartitionSpec as P

EPS = 1e-05
STEP = 16
NEG = -1e30


def norm_stats(x):
    center = x - jnp.mean(x, axis=-1, keepdims=True)
    scale = lax.rsqrt(jnp.mean(center * center, axis=-1, keepdims=True) + EPS)
    return center * scale, scale


def norm_back(g, s, scale, gain):
    q = g * gain
    gx = (q - jnp.mean(q, axis=-1, keepdims=True) - s * jnp.mean(q * s, axis=-1, keepdims=True)) * scale
    return gx, jnp.sum(g * s, axis=0), jnp.sum(g, axis=0)


def blended(now, before, mix):
    return (now.astype(jnp.float32) * mix + before.astype(jnp.float32) * (1.0 - mix)).astype(jnp.bfloat16)


def dot_nt(x, y):
    return lax.dot_general(x, y, (((1,), (1,)), ((), ())), preferred_element_type=jnp.float32)


def dot_nn(x, y):
    return lax.dot_general(x, y, (((1,), (0,)), ((), ())), preferred_element_type=jnp.float32)


def dot_tn(x, y):
    return lax.dot_general(x, y, (((0,), (0,)), ((), ())), preferred_element_type=jnp.float32)


LANES = 128
VMEM = pl.BlockSpec(memory_space=pltpu.VMEM)


def scan_groups(width):
    blocks = width // LANES
    size = 4 if blocks % 4 == 0 else 1
    return [range(g, g + size) for g in range(0, blocks, size)]


def lane(c):
    return slice(c * LANES, (c + 1) * LANES)


def wkv_forward_body(k_ref, v_ref, r_ref, w_ref, u_ref, a0_ref, b0_ref, m0_ref,
                     g_ref, kb, vb, yb, mb, ab, bb, sm, sa, sb):
    rows, width = k_ref.shape
    chunks = rows // STEP
    for c in range(width // LANES):
        kb[c] = k_ref[:, lane(c)]
        vb[c] = v_ref[:, lane(c)]

    for group in scan_groups(width):
        m = [jnp.full((chunks, LANES), NEG, jnp.float32) for _ in group]
        a = [jnp.zeros((chunks, LANES), jnp.float32) for _ in group]
        b = [jnp.zeros((chunks, LANES), jnp.float32) for _ in group]
        for j in range(STEP):
            at = pl.ds(j, chunks, stride=STEP)
            for i, c in enumerate(group):
                k = kb[c, at, :]
                mw = m[i] - w_ref[:, lane(c)]
                m[i] = jnp.maximum(mw, k)
                keep = jnp.exp(mw - m[i])
                take = jnp.exp(k - m[i])
                a[i] = keep * a[i] + take * vb[c, at, :]
                b[i] = keep * b[i] + take
        for i, c in enumerate(group):
            sm[:, lane(c)] = m[i]
            sa[:, lane(c)] = a[i]
            sb[:, lane(c)] = b[i]

    w = w_ref[...]
    m, a, b = m0_ref[...], a0_ref[...], b0_ref[...]
    for s in range(chunks):
        me, ae, be = sm[s:s + 1, :], sa[s:s + 1, :], sb[s:s + 1, :]
        sm[s:s + 1, :] = m
        sa[s:s + 1, :] = a
        sb[s:s + 1, :] = b
        mw = m - float(STEP) * w
        m = jnp.maximum(mw, me)
        keep = jnp.exp(mw - m)
        take = jnp.exp(me - m)
        a = keep * a + take * ae
        b = keep * b + take * be

    for group in scan_groups(width):
        m = [sm[:, lane(c)] for c in group]
        a = [sa[:, lane(c)] for c in group]
        b = [sb[:, lane(c)] for c in group]
        for j in range(STEP):
            at = pl.ds(j, chunks, stride=STEP)
            for i, c in enumerate(group):
                k = kb[c, at, :]
                v = vb[c, at, :]
                mb[c, at, :] = m[i]
                ab[c, at, :] = a[i]
                bb[c, at, :] = b[i]
                uk = u_ref[:, lane(c)] + k
                p = jnp.maximum(m[i], uk)
                alpha = jnp.exp(m[i] - p)
                beta = jnp.exp(uk - p)
                yb[c, at, :] = (alpha * a[i] + beta * v) / (alpha * b[i] + beta)
                mw = m[i] - w_ref[:, lane(c)]
                m[i] = jnp.maximum(mw, k)
                keep = jnp.exp(mw - m[i])
                take = jnp.exp(k - m[i])
                a[i] = keep * a[i] + take * v
                b[i] = keep * b[i] + take
    for c in range(width // LANES):
        g_ref[:, lane(c)] = (jax.nn.sigmoid(r_ref[:, lane(c)]) * yb[c]).astype(jnp.bfloat16)


def wkv_forward(k, v, r, w, u, a0, b0, m0):
    rows, width = k.shape
    block = jax.ShapeDtypeStruct((width // LANES, rows, LANES), jnp.float32)
    chunks = rows // STEP
    return pl.pallas_call(
        wkv_forward_body,
        out_shape=(jax.ShapeDtypeStruct((rows, width), jnp.bfloat16),) + (block,) * 6,
        in_specs=[VMEM] * 8,
        out_specs=[VMEM] * 7,
        scratch_shapes=[pltpu.VMEM((chunks, width), jnp.float32)] * 3,
        compiler_params=pltpu.CompilerParams(vmem_limit_bytes=40 * 2**20),
        cost_estimate=pl.CostEstimate(flops=60 * rows * width, transcendentals=7 * rows * width, bytes_accessed=36 * rows * width),
        name="wkv_forward",
    )(k, v, r, w, u, a0, b0, m0)


def wkv_carry_body(r_ref, gg_ref, kb, yb, mb, bb, w_ref, u_ref, gyb, ca_ref, cb_ref, lc_ref, la_ref, lb_ref, lg_ref):
    rows, width = r_ref.shape
    chunks = rows // STEP
    for c in range(width // LANES):
        gyb[c] = gg_ref[:, lane(c)] * jax.nn.sigmoid(r_ref[:, lane(c)])
    for group in scan_groups(width):
        ga = [jnp.zeros((chunks, LANES), jnp.float32) for _ in group]
        gb = [jnp.zeros((chunks, LANES), jnp.float32) for _ in group]
        end = [None for _ in group]
        for j in reversed(range(STEP)):
            at = pl.ds(j, chunks, stride=STEP)
            for i, c in enumerate(group):
                w = w_ref[:, lane(c)]
                k = kb[c, at, :]
                m = mb[c, at, :]
                uk = u_ref[:, lane(c)] + k
                p = jnp.maximum(m, uk)
                alpha = jnp.exp(m - p)
                beta = jnp.exp(uk - p)
                gn = gyb[c, at, :] / (alpha * bb[c, at, :] + beta)
                gd = -gn * yb[c, at, :]
                mw = m - w
                mn = jnp.maximum(mw, k)
                if j == STEP - 1:
                    end[i] = mn
                keep = jnp.exp(mw - mn)
                ga[i] = alpha * gn + keep * ga[i]
                gb[i] = alpha * gd + keep * gb[i]
                if j == 0:
                    lc_ref[:, lane(c)] = m - float(STEP) * w - end[i]
        for i, c in enumerate(group):
            ca_ref[:, lane(c)] = ga[i]
            cb_ref[:, lane(c)] = gb[i]
    ga = jnp.zeros((1, width), jnp.float32)
    gb = jnp.zeros((1, width), jnp.float32)
    lg = jnp.zeros((1, width), jnp.float32)
    for s in reversed(range(chunks)):
        keep = jnp.exp(lc_ref[s:s + 1, :])
        ga = ca_ref[s:s + 1, :] + keep * ga
        gb = cb_ref[s:s + 1, :] + keep * gb
        lg = lg + lc_ref[s:s + 1, :]
    la_ref[...] = ga
    lb_ref[...] = gb
    lg_ref[...] = lg


def wkv_carry(r, gg, kb, yb, mb, bb, w, u):
    rows, width = r.shape
    chunks = rows // STEP
    small = jax.ShapeDtypeStruct((chunks, width), jnp.float32)
    row = jax.ShapeDtypeStruct((1, width), jnp.float32)
    block = jax.ShapeDtypeStruct((width // LANES, rows, LANES), jnp.float32)
    return pl.pallas_call(
        wkv_carry_body,
        out_shape=(block, small, small, small, row, row, row),
        in_specs=[VMEM] * 8,
        out_specs=[VMEM] * 7,
        compiler_params=pltpu.CompilerParams(vmem_limit_bytes=40 * 2**20),
        cost_estimate=pl.CostEstimate(flops=40 * rows * width, transcendentals=5 * rows * width, bytes_accessed=28 * rows * width),
        name="wkv_carry",
    )(r, gg, kb, yb, mb, bb, w, u)


def wkv_backward_body(r_ref, gg_ref, kb, vb, yb, mb, ab, bb, gyb, w_ref, u_ref, ca_ref, cb_ref, lc_ref, ea_ref, eb_ref,
                      gk_ref, gv_ref, gr_ref, gu_ref, gw_ref, ta, tb, fk, fv):
    rows, width = r_ref.shape
    chunks = rows // STEP
    ga, gb = ea_ref[...], eb_ref[...]
    for s in reversed(range(chunks)):
        ta[s:s + 1, :] = ga
        tb[s:s + 1, :] = gb
        keep = jnp.exp(lc_ref[s:s + 1, :])
        ga = ca_ref[s:s + 1, :] + keep * ga
        gb = cb_ref[s:s + 1, :] + keep * gb
    for group in scan_groups(width):
        ga = [ta[:, lane(c)] for c in group]
        gb = [tb[:, lane(c)] for c in group]
        gu = [jnp.zeros((chunks, LANES), jnp.float32) for _ in group]
        gw = [jnp.zeros((chunks, LANES), jnp.float32) for _ in group]
        for j in reversed(range(STEP)):
            at = pl.ds(j, chunks, stride=STEP)
            for i, c in enumerate(group):
                k = kb[c, at, :]
                v = vb[c, at, :]
                m = mb[c, at, :]
                uk = u_ref[:, lane(c)] + k
                p = jnp.maximum(m, uk)
                alpha = jnp.exp(m - p)
                beta = jnp.exp(uk - p)
                b = bb[c, at, :]
                gn = gyb[c, at, :] / (alpha * b + beta)
                gd = -gn * yb[c, at, :]
                mw = m - w_ref[:, lane(c)]
                mn = jnp.maximum(mw, k)
                keep = jnp.exp(mw - mn)
                take = jnp.exp(k - mn)
                now = beta * (gn * v + gd)
                fv[c, at, :] = beta * gn + take * ga[i]
                fk[c, at, :] = now + take * (ga[i] * v + gb[i])
                gu[i] = gu[i] + now
                gw[i] = gw[i] + keep * (ga[i] * ab[c, at, :] + gb[i] * b)
                ga[i] = alpha * gn + keep * ga[i]
                gb[i] = alpha * gd + keep * gb[i]
        for i, c in enumerate(group):
            gu_ref[:, lane(c)] = jnp.sum(gu[i], axis=0, keepdims=True)
            gw_ref[:, lane(c)] = -jnp.sum(gw[i], axis=0, keepdims=True)
    for c in range(width // LANES):
        gk_ref[:, lane(c)] = fk[c].astype(jnp.bfloat16)
        gv_ref[:, lane(c)] = fv[c].astype(jnp.bfloat16)
        sig = jax.nn.sigmoid(r_ref[:, lane(c)])
        gr_ref[:, lane(c)] = (gg_ref[:, lane(c)] * yb[c] * sig * (1.0 - sig)).astype(jnp.bfloat16)


def wkv_backward(r, gg, kb, vb, yb, mb, ab, bb, gyb, w, u, ca, cb, lc, ea, eb):
    rows, width = r.shape
    chunks = rows // STEP
    low = jax.ShapeDtypeStruct((rows, width), jnp.bfloat16)
    row = jax.ShapeDtypeStruct((1, width), jnp.float32)
    return pl.pallas_call(
        wkv_backward_body,
        out_shape=(low, low, low, row, row),
        in_specs=[VMEM] * 16,
        out_specs=[VMEM] * 5,
        scratch_shapes=[pltpu.VMEM((chunks, width), jnp.float32)] * 2 + [pltpu.VMEM((width // LANES, rows, LANES), jnp.float32)] * 2,
        compiler_params=pltpu.CompilerParams(vmem_limit_bytes=40 * 2**20),
        cost_estimate=pl.CostEstimate(flops=80 * rows * width, transcendentals=6 * rows * width, bytes_accessed=44 * rows * width),
        name="wkv_backward",
    )(r, gg, kb, vb, yb, mb, ab, bb, gyb, w, u, ca, cb, lc, ea, eb)


def local(nd, nt, x, num, den, top, prev_a, prev_f, n1g, n1b, fading, reward, mk, mv, mr, wk, wv, wr, wo, n2g, n2b, ck, cr,
          fk, fv, fr, up):
    rows, dim = x.shape
    seqs = prev_a.shape[0]
    span = nt // seqs
    tp = lax.axis_index("tensor")
    dp = lax.axis_index("dp")
    seq = tp // span
    pos = tp % span
    part = dim // nd
    head = num.shape[1]
    ahead = [(i, i + 1) for i in range(nt - 1)]
    behind = [(i + 1, i) for i in range(nt - 1)]

    def gather(shard):
        whole = lax.all_gather(shard.T, ("dp", "tensor"), axis=0, tiled=True)
        return whole.reshape(nd, nt * shard.shape[1], shard.shape[0])

    whole_k, whole_v, whole_r, whole_o = gather(wk), gather(wv), gather(wr), gather(wo)
    whole_fk, whole_fv, whole_fr = gather(fk), gather(fv), gather(fr)
    states = lax.all_gather(jnp.stack([num, den, top]), "tensor", axis=2, tiled=True)

    def into(left, whole):
        total = dot_nt(left[:, :part], whole[0])
        for d in range(1, nd):
            total = total + dot_nt(left[:, d * part:(d + 1) * part], whole[d])
        return total

    def outof(left, whole):
        return jnp.concatenate([dot_nn(left, whole[d]) for d in range(nd)], axis=1)

    def weight_grad(cols, ins):
        both = dot_tn(cols, ins).astype(jnp.bfloat16)
        return jnp.stack([both[:, d * part:(d + 1) * part] for d in range(nd)])

    def prior(rows_now, previous):
        halo = lax.ppermute(rows_now[-1:, :], "tensor", ahead)
        mine = lax.dynamic_slice_in_dim(previous, seq, 1, 0)
        first = jnp.where(pos == 0, mine, halo)
        return jnp.concatenate([first, rows_now[:-1, :]], axis=0)

    def pushed(back):
        halo = lax.ppermute(back[:1, :], "tensor", behind)
        last = jnp.where(pos == span - 1, 0.0, halo)
        return jnp.concatenate([back[1:, :], last], axis=0)

    s1, scale1 = norm_stats(x)
    first = (s1 * n1g + n1b).astype(jnp.bfloat16)
    before = prior(first, prev_a)
    key_in, value_in, recept_in = blended(first, before, mk), blended(first, before, mv), blended(first, before, mr)
    keys, vals, recept = into(key_in, whole_k), into(value_in, whole_v), into(recept_in, whole_r)

    w = jnp.exp(fading)
    steps = jnp.arange(rows, dtype=jnp.float32)[:, None]
    tail = keys - (rows - 1.0 - steps) * w
    m_loc = jnp.max(tail, axis=0)
    e_loc = jnp.exp(tail - m_loc)
    sent = jnp.stack([jnp.sum(e_loc * vals, axis=0), jnp.sum(e_loc, axis=0), m_loc])
    got = lax.all_gather(sent, "tensor", axis=0)
    mine = lax.dynamic_slice_in_dim(got, seq * span, span, 0)
    start = lax.dynamic_index_in_dim(states, seq, 1, keepdims=False)
    a, b, m = start[0], start[1], start[2]
    for i in range(span - 1):
        on = i < pos
        mw = m - rows * w
        mn = jnp.maximum(mw, mine[i, 2])
        keep, take = jnp.exp(mw - mn), jnp.exp(mine[i, 2] - mn)
        a = jnp.where(on, keep * a + take * mine[i, 0], a)
        b = jnp.where(on, keep * b + take * mine[i, 1], b)
        m = jnp.where(on, mn, m)
    wr_, ur_ = w[None, :], reward[None, :]
    gated, kb, vb, yb, mb, ab, bb = wkv_forward(keys, vals, recept, wr_, ur_, a[None, :], b[None, :], m[None, :])
    middle = x + outof(gated, whole_o)

    s2, scale2 = norm_stats(middle)
    second = (s2 * n2g + n2b).astype(jnp.bfloat16)
    before2 = prior(second, prev_f)
    chan_key = blended(second, before2, ck)
    chan_rec = blended(second, before2, cr)
    hidden = jnp.maximum(into(chan_key, whole_fk), 0.0)
    squared = jnp.square(hidden).astype(jnp.bfloat16)
    chan_values = outof(squared, whole_fv)
    gate = jax.nn.sigmoid(into(chan_rec, whole_fr))
    result = middle + gate * chan_values

    g_values = (up * gate).astype(jnp.bfloat16)
    g_gate = (up * chan_values * gate * (1.0 - gate)).astype(jnp.bfloat16)
    grad_fr = weight_grad(g_gate, chan_rec)
    g_rec_in = outof(g_gate, whole_fr)
    g_squared = into(g_values, whole_fv)
    grad_fv = weight_grad(squared, g_values)
    g_hidden = (g_squared * 2.0 * hidden).astype(jnp.bfloat16)
    grad_fk = weight_grad(g_hidden, chan_key)
    g_key_in = outof(g_hidden, whole_fk)
    diff2 = second.astype(jnp.float32) - before2.astype(jnp.float32)
    grad_ck = jnp.sum(g_key_in * diff2, axis=0)
    grad_cr = jnp.sum(g_rec_in * diff2, axis=0)
    back2 = g_key_in * (1.0 - ck) + g_rec_in * (1.0 - cr)
    g_second = g_key_in * ck + g_rec_in * cr + pushed(back2)
    g_mid, grad_g2, grad_b2 = norm_back(g_second, s2, scale2, n2g)
    g_middle = up + g_mid
    g_attn = g_middle.astype(jnp.bfloat16)
    g_gated = into(g_attn, whole_o)
    grad_o = weight_grad(gated, g_attn)

    gyb, ca, cb, lc, la, lb, lg = wkv_carry(recept, g_gated, kb, yb, mb, bb, wr_, ur_)
    sent = jnp.concatenate([la, lb, lg], axis=0)
    got = lax.all_gather(sent, "tensor", axis=0)

    def chain(items, steps_on):
        ga = jnp.zeros((dim,), jnp.float32)
        gb = jnp.zeros((dim,), jnp.float32)
        for i in reversed(range(span)):
            keep = jnp.exp(items[i, 2])
            na, nb = items[i, 0] + keep * ga, items[i, 1] + keep * gb
            if steps_on is None:
                ga, gb = na, nb
            else:
                on = i > steps_on
                ga, gb = jnp.where(on, na, ga), jnp.where(on, nb, gb)
        return ga, gb

    ea, eb = chain(lax.dynamic_slice_in_dim(got, seq * span, span, 0), pos)
    own = lax.dynamic_slice_in_dim(got, tp * head, head, 2)
    nums, dens = [], []
    for s in range(seqs):
        ga, gb = jnp.zeros((head,), jnp.float32), jnp.zeros((head,), jnp.float32)
        for i in reversed(range(span)):
            keep = jnp.exp(own[s * span + i, 2])
            ga, gb = own[s * span + i, 0] + keep * ga, own[s * span + i, 1] + keep * gb
        nums.append(ga)
        dens.append(gb)
    grad_num, grad_den = jnp.stack(nums), jnp.stack(dens)
    grad_top = grad_num * num + grad_den * den

    g_keys, g_vals, g_recept, gu, gw = wkv_backward(
        recept, g_gated, kb, vb, yb, mb, ab, bb, gyb, wr_, ur_, ca, cb, lc, ea[None, :], eb[None, :])
    grad_k, grad_v, grad_r = weight_grad(g_keys, key_in), weight_grad(g_vals, value_in), weight_grad(g_recept, recept_in)
    diff1 = first.astype(jnp.float32) - before.astype(jnp.float32)
    in_k, in_v, in_r = outof(g_keys, whole_k), outof(g_vals, whole_v), outof(g_recept, whole_r)
    grad_mk, grad_mv, grad_mr = jnp.sum(in_k * diff1, axis=0), jnp.sum(in_v * diff1, axis=0), jnp.sum(in_r * diff1, axis=0)
    back1 = in_k * (1.0 - mk) + in_v * (1.0 - mv) + in_r * (1.0 - mr)
    g_first = in_k * mk + in_v * mv + in_r * mr + pushed(back1)
    g_tok, grad_g1, grad_b1 = norm_back(g_first, s1, scale1, n1g)
    tokens_grad = g_middle + g_tok

    def scatter(stack):
        cols = stack.shape[1]
        mine = lax.psum_scatter(stack.reshape(nd * cols, part), "dp", scatter_dimension=0, tiled=True)
        mine = lax.psum_scatter(mine, "tensor", scatter_dimension=0, tiled=True)
        return mine.astype(jnp.float32).T

    out_k, out_v, out_r, out_o = scatter(grad_k), scatter(grad_v), scatter(grad_r), scatter(grad_o)
    out_fk, out_fv, out_fr = scatter(grad_fk), scatter(grad_fv), scatter(grad_fr)

    vectors = jnp.stack([grad_g1, grad_b1, gw[0] * w, gu[0], grad_mk, grad_mv, grad_mr, grad_g2, grad_b2, grad_ck, grad_cr])
    lead = jnp.where(pos == 0, 1.0, 0.0)
    slots = jnp.zeros((2, nd, seqs, dim), jnp.float32)
    pair = (jnp.stack([back1[0], back2[0]]) * lead)[:, None, None, :]
    slots = lax.dynamic_update_slice(slots, pair, (0, dp, seq, 0))
    vectors, slots = lax.psum((vectors, slots), ("dp", "tensor"))
    prevs = lax.dynamic_index_in_dim(slots, dp, axis=1, keepdims=False)
    return (result, tokens_grad, grad_num, grad_den, grad_top, prevs[0], prevs[1],
            vectors[0], vectors[1], vectors[2], vectors[3], vectors[4], vectors[5], vectors[6],
            out_k, out_v, out_r, out_o, vectors[7], vectors[8], vectors[9], vectors[10], out_fk, out_fv, out_fr)


def solution(mesh):
    nd, nt = mesh.shape["dp"], mesh.shape["tensor"]
    rows, both, lead, one = P(("dp", "tensor"), None), P("dp", "tensor"), P("dp", None), P()
    return jax.shard_map(
        functools.partial(local, nd, nt),
        mesh=mesh,
        in_specs=(rows, both, both, both, lead, lead) + (one,) * 7 + (both,) * 4 + (one,) * 4 + (both,) * 3 + (rows,),
        out_specs=(rows, rows, both, both, both, lead, lead) + (one,) * 7 + (both,) * 4 + (one,) * 4 + (both,) * 3,
        check_vma=False,
    )
```

time: 3450 us -> 1390 us (0.40)
  waiting for transfers between devices: 1850 us -> 1020 us
  other arithmetic: 819 us -> 56.5 us
  local copies, waits for them, and re-layouts: 541 us -> 60.3 us
  blocking collectives: 15.6 us -> 128 us
  matrix products: 169 us -> 77.7 us
    reduce_scatter x12 -> x14, waiting for transfers between devices: 1280 us -> 565 us  [the longest x7 565 us: scatter(): mine = lax.psum_scatter(mine, 'tensor', scatter_dimension=0, tiled=True)]
    reduce_sum x266 -> x8, other arithmetic: 405 us -> 11.2 us  [the longest x2 5.15 us: norm_back(): return (gx, jnp.sum(g * s, axis=0), jnp.sum(g, axis=0))]
    dynamic_update_slice x162 -> x1, local copies, waits for them, and re-layouts: 206 us -> 0.07 us  [local(): slots = lax.dynamic_update_slice(slots, pair, (0, dp, seq, 0))]
    squeeze x257 -> x1, local copies, waits for them, and re-layouts: 185 us -> 1.32 us  [local(): prevs[1]]
    reduce_max x96 -> x0, other arithmetic: 175 us -> none  [the longest x64 172 us: span_blend(): highest = jnp.maximum(jnp.max(scores, axis=1), carried)]
    all_gather x5 -> x7, waiting for transfers between devices: 455 us -> 320 us  [gather(): whole = lax.all_gather(shard.T, ('dp', 'tensor'), axis=0, tiled=True)]
    all_gather x7 -> x3, blocking collectives: 15.6 us -> 128 us  [the longest x2 80.6 us: local(): got = lax.all_gather(sent, 'tensor', axis=0)]
    dot_general x21 -> x35, matrix products: 169 us -> 77.7 us  [the longest x14 36.8 us: dot_nt(): lax.dot_general(x, y, (((1,), (1,)), ((), ())), preferred_element_type=jn...]
  transfers between devices with their start and end apart: 18 -> 26, of which waited for: 11 -> 17; matrix products, arithmetic and copies ran while one was open for 22% -> 12% of each run, Pallas kernels for 0% -> 1%
where the time goes in v1:
time: 1390 us; the launch traced here: 1380 us
  waiting for transfers between devices  1020 us (73%)
  blocking collectives  128 us (9%)
  matrix products  77.7 us (6%)
  local copies, waits for them, and re-layouts  60.3 us (4%)
  other arithmetic  56.5 us (4%)
  between operations  16.4 us (1%)
    reduce_scatter x7, waiting for transfers between devices, scatter(): mine = lax.psum_scatter(mine, 'tensor', scatter_dimension=0, tiled=True)  565 us
    all_gather x7, waiting for transfers between devices, gather(): whole = lax.all_gather(shard.T, ('dp', 'tensor'), axis=0, tiled=True)  320 us
    psum x1, waiting for transfers between devices, local(): vectors, slots = lax.psum((vectors, slots), ('dp', 'tensor'))  117 us
    all_gather x2, blocking collectives, local(): got = lax.all_gather(sent, 'tensor', axis=0)  80.6 us
    all_gather x1, blocking collectives, local(): lax.all_gather(jnp.stack([num, den, top]), 'tensor', axis=2, tiled=True)  47.6 us
    dot_general x14, matrix products, dot_nt(): lax.dot_general(x, y, (((1,), (1,)), ((), ())), preferred_element_type=jn...  36.8 us
  transfers between devices with their start and end apart: 26, of which 17 were waited for; matrix products, arithmetic and copies ran while one was open for 12% of the time, Pallas kernels for 1%

profile of v1, /device:TPU:0, one launch (start us, length us, event | category | flops | bytes accessed | tf_op | source)
XLA Modules:
  0.0 1379.8 jit_solution(6799023642519137841)
XLA Ops:
  16.5 4.8 collective-permute-start
  21.5 47.6 %all_gather.39 = f32[3,2,1024]{0,1,2:T(2,128)S(1)} all-gather(f32[3,2,64]{0,1,2:T(2,128)S(1)} %copy.55), channel_id=1, replica_groups=mesh['dp'=2,'tensor'=16] {'tensor'}, dimensions={2}, use_global_device_ids=true | all-gather | bytes 26112 | tf_op jit(solution)/shard_map/all_gather | solution.py:291
  69.1 11.0 dynamic-slice_reduce_fusion
  82.1 3.0 fusion.59
  85.2 46.7 %all-gather.12.cloned.1.call-done = bf16[2048,512]{1,0:T(8,128)(2,1)} async-done(((bf16[64,512]{1,0:T(8,128)(2,1)}), bf16[2048,512]{1,0:T(8,128)(2,1)}) %all-gather.12.cloned.1.call-update) | async-done | bytes 2097168 | tf_op jit(solution)/shard_map/all_gather | solution.py:286
  135.6 2.5 multiply_reduce_fusion.10
  138.1 40.9 %all-gather.2 = f32[16,3,1024]{2,1,0:T(4,128)S(1)} all-gather(f32[1,3,1024]{2,1,0:T(4,128)S(1)} %maximum_bitcast_fusion), channel_id=2, replica_groups=mesh['dp'=2,'tensor'=16] {'tensor'}, dimensions={0}, use_global_device_ids=true | all-gather | bytes 208896 | tf_op jit(solution)/shard_map/all_gather | solution.py:329
  179.2 11.1 all-gather.16.cloned.1.call-done
  193.8 3.4 wkv_forward.1
  203.1 45.1 %all-gather.18.cloned.1.call-done = bf16[2048,512]{1,0:T(8,128)(2,1)} async-done(((bf16[64,512]{1,0:T(8,128)(2,1)}), bf16[2048,512]{1,0:T(8,128)(2,1)}) %all-gather.18.cloned.1.call-update) | async-done | bytes 2097168 | tf_op jit(solution)/shard_map/all_gather | solution.py:286
  253.9 3.3 collective-permute-start.1
  260.3 45.9 %all-gather.20.cloned.1.call-done = bf16[2048,512]{1,0:T(8,128)(2,1)} async-done(((bf16[64,512]{1,0:T(8,128)(2,1)}), bf16[2048,512]{1,0:T(8,128)(2,1)}) %all-gather.20.cloned.1.call-update) | async-done | bytes 2097168 | tf_op jit(solution)/shard_map/all_gather | solution.py:286
  306.2 2.8 fusion.38
  309.0 88.9 %all-gather.22.cloned.1.call-done = bf16[8192,512]{0,1:T(8,128)(2,1)} async-done(((bf16[256,512]{0,1:T(8,128)(2,1)}), bf16[8192,512]{0,1:T(8,128)(2,1)}) %all-gather.22.cloned.1.call-update) | async-done | bytes 8388624 | tf_op jit(solution)/shard_map/all_gather | solution.py:286
  397.9 3.7 fusion.16
  402.6 4.2 fusion.1
  406.9 82.3 %all-gather.24.cloned.1.call-done = bf16[8192,512]{0,1:T(8,128)(2,1)} async-done(((bf16[256,512]{0,1:T(8,128)(2,1)}), bf16[8192,512]{0,1:T(8,128)(2,1)}) %all-gather.24.cloned.1.call-update) | async-done | bytes 8388624 | tf_op jit(solution)/shard_map/all_gather | solution.py:286
  489.1 4.9 fusion.5
  494.1 3.7 fusion.9
  505.2 2.0 fusion.36
  507.2 3.7 fusion.7
  511.2 4.1 fusion.3
  522.4 2.8 collective-permute-done.2
  525.1 2.3 multiply_reduce_fusion.2
  535.2 2.5 wkv_carry.1
  537.7 39.7 %all-gather.3 = f32[16,3,1024]{2,1,0:T(4,128)S(1)} all-gather(f32[1,3,1024]{2,1,0:T(4,128)S(1)} %maximum_bitcast_fusion.1), channel_id=3, replica_groups=mesh['dp'=2,'tensor'=16] {'tensor'}, dimensions={0}, use_global_device_ids=true | all-gather | bytes 208896 | tf_op jit(solution)/shard_map/all_gather | solution.py:378
  577.5 4.9 wkv_backward.1
  591.3 4.6 convolution_convert_fusion
  595.9 3.9 slice_bitcast_fusion.1
  599.8 7.8 pad_maximum_fusion.1
  607.6 11.5 copy.57
  620.2 4.0 convolution_convert_fusion.1
  624.2 4.3 slice_bitcast_fusion.3
  628.5 9.6 pad_maximum_fusion
  638.0 11.5 copy.56
  651.4 2.1 fusion.64
  653.6 2.0 fusion.54
  655.6 2.1 fusion.57
  662.2 2.9 collective-permute-done.3
  665.2 2.9 multiply_reduce_fusion.6
  676.1 117.2 %all-reduce.3.cloned.1.call-done = (f32[2,2,2,1024]{3,2,1,0:T(2,128)}, f32[11,1024]{1,0:T(8,128)}) async-done(((f32[2,2,2,1024]{3,2,1,0:T(2,128)}, f32[11,1024]{1,0:T(8,128)}), (f32[2,2,2,1024]{3,2,1,0:T(2,128)}, f32[11,1024]{1,0:T(8,128)})) %all-reduce.3.cloned.1.call-update) | async-done | bytes 77840 | tf_op jit(solution)/shard_map/psum | solution.py:431
  796.5 77.7 %reduce-scatter.41.cloned.1.call-done = bf16[64,512]{1,0:T(8,128)(2,1)} async-done(((bf16[1024,512]{1,0:T(8,128)(2,1)}), bf16[64,512]{1,0:T(8,128)(2,1)}) %reduce-scatter.41.cloned.1.call-update) | async-done | bytes 65552 | tf_op jit(solution)/shard_map/reduce_scatter | solution.py:420
  875.7 74.6 %reduce-scatter.29.cloned.1.call-done = bf16[64,512]{1,0:T(8,128)(2,1)} async-done(((bf16[1024,512]{1,0:T(8,128)(2,1)}), bf16[64,512]{1,0:T(8,128)(2,1)}) %reduce-scatter.29.cloned.1.call-update) | async-done | bytes 65552 | tf_op jit(solution)/shard_map/reduce_scatter | solution.py:420
  951.8 75.0 %reduce-scatter.25.cloned.1.call-done = bf16[64,512]{1,0:T(8,128)(2,1)} async-done(((bf16[1024,512]{1,0:T(8,128)(2,1)}), bf16[64,512]{1,0:T(8,128)(2,1)}) %reduce-scatter.25.cloned.1.call-update) | async-done | bytes 65552 | tf_op jit(solution)/shard_map/reduce_scatter | solution.py:420
  1028.3 74.9 %reduce-scatter.21.cloned.1.call-done = bf16[64,512]{1,0:T(8,128)(2,1)} async-done(((bf16[1024,512]{1,0:T(8,128)(2,1)}), bf16[64,512]{1,0:T(8,128)(2,1)}) %reduce-scatter.21.cloned.1.call-update) | async-done | bytes 65552 | tf_op jit(solution)/shard_map/reduce_scatter | solution.py:420
  1104.8 75.0 %reduce-scatter.17.cloned.1.call-done = bf16[64,512]{1,0:T(8,128)(2,1)} async-done(((bf16[1024,512]{1,0:T(8,128)(2,1)}), bf16[64,512]{1,0:T(8,128)(2,1)}) %reduce-scatter.17.cloned.1.call-update) | async-done | bytes 65552 | tf_op jit(solution)/shard_map/reduce_scatter | solution.py:420
  1181.3 92.4 %reduce-scatter.37.cloned.1.call-done = bf16[256,512]{0,1:T(8,128)(2,1)} async-done(((bf16[4096,512]{0,1:T(8,128)(2,1)}), bf16[256,512]{0,1:T(8,128)(2,1)}) %reduce-scatter.37.cloned.1.call-update) | async-done | bytes 262160 | tf_op jit(solution)/shard_map/reduce_scatter | solution.py:420
  1275.4 95.3 %reduce-scatter.33.cloned.1.call-done = bf16[256,512]{0,1:T(8,128)(2,1)} async-done(((bf16[4096,512]{0,1:T(8,128)(2,1)}), bf16[256,512]{0,1:T(8,128)(2,1)}) %reduce-scatter.33.cloned.1.call-update) | async-done | bytes 262160 | tf_op jit(solution)/shard_map/reduce_scatter | solution.py:420
  (306 shorter events, 94.2 us)
Async XLA Ops:
  7.2 73.1 %copy-start.20 = (f32[256,1024]{1,0:T(8,128)S(1)}, f32[256,1024]{1,0:T(8,128)}, u32[]{:S(2)}) copy-start(f32[256,1024]{1,0:T(8,128)} %param.25) | copy-start | bytes 3145732
  7.2 73.1 %copy-start.64 = (f32[1024]{0:T(1024)S(1)}, f32[1024]{0:T(1024)}, u32[]{:S(2)}) copy-start(f32[1024]{0:T(1024)} %param.31) | copy-start | bytes 12292
  7.2 73.1 %copy-start.66 = (f32[1024]{0:T(1024)S(1)}, f32[1024]{0:T(1024)}, u32[]{:S(2)}) copy-start(f32[1024]{0:T(1024)} %param.32) | copy-start | bytes 12292
  7.2 14.1 %copy-start.75 = (f32[2,64]{1,0:T(2,128)S(1)}, f32[2,64]{1,0:T(2,128)}, u32[]{:S(2)}) copy-start(f32[2,64]{1,0:T(2,128)} %param.26) | copy-start | bytes 1540
  7.3 14.1 %copy-start.74 = (f32[2,64]{1,0:T(2,128)S(1)}, f32[2,64]{1,0:T(2,128)}, u32[]{:S(2)}) copy-start(f32[2,64]{1,0:T(2,128)} %param.27) | copy-start | bytes 1540
  7.3 14.1 %copy-start.76 = (f32[2,64]{1,0:T(2,128)S(1)}, f32[2,64]{1,0:T(2,128)}, u32[]{:S(2)}) copy-start(f32[2,64]{1,0:T(2,128)} %param.28) | copy-start | bytes 1540
  7.3 72.8 %copy-start.67 = (f32[1024]{0:T(1024)S(1)}, f32[1024]{0:T(1024)}, u32[]{:S(2)}) copy-start(f32[1024]{0:T(1024)} %param.35) | copy-start | bytes 12292
  7.3 72.9 %copy-start.68 = (f32[1024]{0:T(1024)S(1)}, f32[1024]{0:T(1024)}, u32[]{:S(2)}) copy-start(f32[1024]{0:T(1024)} %param.37) | copy-start | bytes 12292
  7.3 72.9 %copy-start.69 = (f32[1024]{0:T(1024)S(1)}, f32[1024]{0:T(1024)}, u32[]{:S(2)}) copy-start(f32[1024]{0:T(1024)} %param.36) | copy-start | bytes 12292
  7.3 72.9 %copy-start.62 = (f32[1024]{0:T(1024)S(1)}, f32[1024]{0:T(1024)}, u32[]{:S(2)}) copy-start(f32[1024]{0:T(1024)} %param.33) | copy-start | bytes 12292
  7.3 72.9 %copy-start.72 = (bf16[2,1024]{1,0:T(2,128)(2,1)S(1)}, bf16[2,1024]{1,0:T(2,128)(2,1)}, u32[]{:S(2)}) copy-start(bf16[2,1024]{1,0:T(2,128)(2,1)} %param.29) | copy-start | bytes 12292
  7.3 74.8 %all-gather.14.cloned.1.call-start = ((), (), s32[]{:S(2)}) async-start(), calls=%async_computation.15 | async-start | bytes 2162688 | tf_op jit(solution)/shard_map/all_gather | solution.py:286
  8.1 123.8 %all-gather.12.cloned.1.call-start = ((), (), s32[]{:S(2)}) async-start(), calls=%async_computation.14 | async-start | bytes 2162688 | tf_op jit(solution)/shard_map/all_gather | solution.py:286
  8.8 181.4 %all-gather.16.cloned.1.call-start = ((), (), s32[]{:S(2)}) async-start(), calls=%async_computation.16 | async-start | bytes 2162688 | tf_op jit(solution)/shard_map/all_gather | solution.py:286
  9.5 238.7 %all-gather.18.cloned.1.call-start = ((), (), s32[]{:S(2)}) async-start(), calls=%async_computation.17 | async-start | bytes 2162688 | tf_op jit(solution)/shard_map/all_gather | solution.py:286
  10.1 296.1 %all-gather.20.cloned.1.call-start = ((), (), s32[]{:S(2)}) async-start(), calls=%async_computation.18 | async-start | bytes 2162688 | tf_op jit(solution)/shard_map/all_gather | solution.py:286
  10.7 387.2 %all-gather.22.cloned.1.call-start = ((), (), s32[]{:S(2)}) async-start(), calls=%async_computation.19 | async-start | bytes 8650752 | tf_op jit(solution)/shard_map/all_gather | solution.py:286
  11.3 477.9 %all-gather.24.cloned.1.call-start = ((), (), s32[]{:S(2)}) async-start(), calls=%async_computation.20 | async-start | bytes 8650752 | tf_op jit(solution)/shard_map/all_gather | solution.py:286
  12.0 657.4 %reduce-scatter.39.cloned.1.call-start = ((), (), s32[]{:S(2)}) async-start(), calls=%async_computation.33 | async-start | bytes 3145728 | tf_op jit(solution)/shard_map/reduce_scatter | solution.py:419
  16.4 68.7 %copy-start.26 = (bf16[256,1024]{1,0:T(8,128)(2,1)}, bf16[256,1024]{1,0:T(8,128)(2,1)S(1)}, u32[]{:S(2)}) copy-start(bf16[256,1024]{1,0:T(8,128)(2,1)S(1)} %add_convert_fusion.1) | copy-start | bytes 1572868
  16.5 63.8 %collective-permute-start = (bf16[1,1024]{1,0:T(2,128)(2,1)S(1)}, bf16[1,1024]{1,0:T(2,128)(2,1)S(1)}, u32[]{:S(2)}, u32[]{:S(2)}) collective-permute-start(bf16[1,1024]{1,0:T(2,128)(2,1)S(1)} %slice.678), channel_id=1, source_target_pairs={{0,1},{1,2},{2,3},{3,4},{4,5},{5,6},{6,7},{7,8},{8,9},{9,10},{10,1... | collective-permute-start | bytes 6152 | tf_op jit(solution)/shard_map/ppermute | solution.py:307
  82.1 49.8 %copy-start.33 = (bf16[256,1024]{1,0:T(8,128)(2,1)}, bf16[256,1024]{1,0:T(8,128)(2,1)S(1)}, u32[]{:S(2)}) copy-start(bf16[256,1024]{1,0:T(8,128)(2,1)S(1)} %get-tuple-element.116) | copy-start | bytes 1572868
  82.1 55.9 %copy-start.31 = (bf16[256,1024]{1,0:T(8,128)(2,1)}, bf16[256,1024]{1,0:T(8,128)(2,1)S(1)}, u32[]{:S(2)}) copy-start(bf16[256,1024]{1,0:T(8,128)(2,1)S(1)} %get-tuple-element.117) | copy-start | bytes 1572868
  133.7 56.5 %copy-start.36 = (bf16[256,1024]{1,0:T(8,128)(2,1)S(1)}, bf16[256,1024]{1,0:T(8,128)(2,1)}, u32[]{:S(2)}) copy-start(bf16[256,1024]{1,0:T(8,128)(2,1)} %get-tuple-element.115) | copy-start | bytes 1572868
  138.1 55.8 %copy-start.19 = (f32[1024]{0:T(1024)S(1)}, f32[1024]{0:T(1024)}, u32[]{:S(2)}) copy-start(f32[1024]{0:T(1024)} %param.34) | copy-start | bytes 12292
  250.1 8.5 copy-start.73
  253.9 4.7 collective-permute-start.1
  503.1 166.9 %reduce-scatter.27.cloned.1.call-start = ((), (), s32[]{:S(2)}) async-start(), calls=%async_computation.27 | async-start | bytes 3145728 | tf_op jit(solution)/shard_map/reduce_scatter | solution.py:419
  505.2 12.8 copy-start.50
  507.2 10.8 copy-start.51
  519.6 5.5 collective-permute-start.2
  531.3 139.3 %reduce-scatter.23.cloned.1.call-start = ((), (), s32[]{:S(2)}) async-start(), calls=%async_computation.25 | async-start | bytes 3145728 | tf_op jit(solution)/shard_map/reduce_scatter | solution.py:419
  535.1 42.4 %copy-start.7 = (f32[8,256,128]{2,1,0:T(8,128)S(1)}, f32[8,256,128]{2,1,0:T(8,128)}, u32[]{:S(2)}) copy-start(f32[8,256,128]{2,1,0:T(8,128)} %copy-done.6) | copy-start | bytes 3145732
  535.1 42.4 %copy-start.9 = (f32[8,256,128]{2,1,0:T(8,128)S(1)}, f32[8,256,128]{2,1,0:T(8,128)}, u32[]{:S(2)}) copy-start(f32[8,256,128]{2,1,0:T(8,128)} %copy-done.8) | copy-start | bytes 3145732
  584.9 86.3 %reduce-scatter.19.cloned.1.call-start = ((), (), s32[]{:S(2)}) async-start(), calls=%async_computation.23 | async-start | bytes 3145728 | tf_op jit(solution)/shard_map/reduce_scatter | solution.py:419
  588.5 83.5 %reduce-scatter.15.cloned.1.call-start = ((), (), s32[]{:S(2)}) async-start(), calls=%async_computation.21 | async-start | bytes 3145728 | tf_op jit(solution)/shard_map/reduce_scatter | solution.py:419
  591.0 81.5 %reduce-scatter.35.cloned.1.call-start = ((), (), s32[]{:S(2)}) async-start(), calls=%async_computation.31 | async-start | bytes 12582912 | tf_op jit(solution)/shard_map/reduce_scatter | solution.py:419
  619.2 54.0 %reduce-scatter.31.cloned.1.call-start = ((), (), s32[]{:S(2)}) async-start(), calls=%async_computation.29 | async-start | bytes 12582912 | tf_op jit(solution)/shard_map/reduce_scatter | solution.py:419
  649.5 143.8 %all-reduce.3.cloned.1.call-start = ((), (), s32[]{:S(2)}) async-start(), calls=%async_computation.35 | async-start | bytes 196608 | tf_op jit(solution)/shard_map/psum | solution.py:431
  649.6 8.1 copy-start.12
  659.7 5.5 collective-permute-start.3
  669.4 204.9 %reduce-scatter.41.cloned.1.call-start = ((), (), s32[]{:S(2)}) async-start(), calls=%async_computation.34 | async-start | bytes 1114112 | tf_op jit(solution)/shard_map/reduce_scatter | solution.py:420
  669.9 280.4 %reduce-scatter.29.cloned.1.call-start = ((), (), s32[]{:S(2)}) async-start(), calls=%async_computation.28 | async-start | bytes 1114112 | tf_op jit(solution)/shard_map/reduce_scatter | solution.py:420
  670.5 356.3 %reduce-scatter.25.cloned.1.call-start = ((), (), s32[]{:S(2)}) async-start(), calls=%async_computation.26 | async-start | bytes 1114112 | tf_op jit(solution)/shard_map/reduce_scatter | solution.py:420
  671.1 432.2 %reduce-scatter.21.cloned.1.call-start = ((), (), s32[]{:S(2)}) async-start(), calls=%async_computation.24 | async-start | bytes 1114112 | tf_op jit(solution)/shard_map/reduce_scatter | solution.py:420
  671.8 507.9 %reduce-scatter.17.cloned.1.call-start = ((), (), s32[]{:S(2)}) async-start(), calls=%async_computation.22 | async-start | bytes 1114112 | tf_op jit(solution)/shard_map/reduce_scatter | solution.py:420
  672.4 601.2 %reduce-scatter.37.cloned.1.call-start = ((), (), s32[]{:S(2)}) async-start(), calls=%async_computation.32 | async-start | bytes 4456448 | tf_op jit(solution)/shard_map/reduce_scatter | solution.py:420
  673.2 697.6 %reduce-scatter.33.cloned.1.call-start = ((), (), s32[]{:S(2)}) async-start(), calls=%async_computation.30 | async-start | bytes 4456448 | tf_op jit(solution)/shard_map/reduce_scatter | solution.py:420
  (57 other events, 200.2 us)
Sparse Core Ops, SparseCore 0:
  11.0 62.3 all-gather.13
  76.3 55.5 all-gather.11
  134.8 55.4 all-gather.15
  193.0 55.1 all-gather.17
  250.9 55.2 all-gather.19
  308.9 88.9 all-gather.21
  400.8 88.3 all-gather.23
  503.2 7.8 reduce-scatter.38
  531.4 10.2 reduce-scatter.26
  585.0 5.4 reduce-scatter.22
  592.9 10.7 reduce-scatter.18
  605.8 10.7 reduce-scatter.14
  619.3 17.6 reduce-scatter.34
  649.6 13.7 reduce-scatter.30
  671.0 122.2 all-reduce.2
  795.5 78.6 reduce-scatter.40
  876.3 73.9 reduce-scatter.28
  952.5 74.2 reduce-scatter.24
  1029.1 74.1 reduce-scatter.20
  1105.4 74.2 reduce-scatter.16
  1182.1 91.5 reduce-scatter.36
  1276.0 94.7 reduce-scatter.32

commit v2 on v1

--- a/solution.py
+++ b/solution.py
@@ -268,6 +268,306 @@
     )(r, gg, kb, vb, yb, mb, ab, bb, gyb, w, u, ca, cb, lc, ea, eb)
 
 
+MESH = pl.DeviceIdType.MESH
+HBM = pl.BlockSpec(memory_space=pltpu.HBM)
+
+
+def place(nd, nz):
+    d = lax.axis_index("dp")
+    t = lax.axis_index("tensor")
+    return d, t // 4, lax.rem(t // 2, 2), lax.rem(t, 2)
+
+
+def spot(d, z, y, x):
+    return (d, z * 4 + y * 2 + x)
+
+
+def partners(nd, nz, d, z, y, x):
+    out = [spot(lax.rem(d + i, nd), z, y, x) for i in range(1, nd)]
+    out += [spot(d, lax.rem(z + i, nz), y, x) for i in range(1, nz)]
+    return out + [spot(d, z, 1 - y, x), spot(d, z, y, 1 - x)]
+
+
+def meet(others):
+    barrier = pltpu.get_barrier_semaphore()
+    for other in others:
+        pl.semaphore_signal(barrier, inc=1, device_id=other, device_id_type=MESH)
+    pl.semaphore_wait(barrier, len(others))
+
+
+def send(src, dst, send_sem, recv_sem, to):
+    return pltpu.make_async_remote_copy(src_ref=src, dst_ref=dst, send_sem=send_sem, recv_sem=recv_sem, device_id=to, device_id_type=MESH)
+
+
+def gather_body(nd, nz, pieces, lag, count, *refs):
+    ins, outs = refs[:count], refs[count:2 * count]
+    loc, zs, zr, as_, ar, bs, br, ds, dr = refs[2 * count:]
+    d, z, y, x = place(nd, nz)
+    meet(partners(nd, nz, d, z, y, x))
+
+    def own(p):
+        a, at, n = pieces[p]
+        return pltpu.make_async_copy(ins[a].at[at:at + n], outs[a].at[d, z, y, x, at:at + n], loc.at[p])
+
+    def along_z(p, i, source):
+        a, at, n = pieces[p]
+        return send(ins[a].at[at:at + n], outs[a].at[d, source, y, x, at:at + n], zs.at[p, i - 1], zr.at[p, i - 1],
+                    spot(d, lax.rem(z + i, nz), y, x))
+
+    def first_pair(p, mine):
+        a, at, n = pieces[p]
+        if p % 2 == 0:
+            part = outs[a].at[d, :, y if mine else 1 - y, x, at:at + n]
+            to = spot(d, z, 1 - y, x)
+        else:
+            part = outs[a].at[d, :, y, x if mine else 1 - x, at:at + n]
+            to = spot(d, z, y, 1 - x)
+        return send(part, part, as_.at[p], ar.at[p], to)
+
+    def second_pair(p, mine):
+        a, at, n = pieces[p]
+        if p % 2 == 0:
+            part = outs[a].at[d, :, :, x if mine else 1 - x, at:at + n]
+            to = spot(d, z, y, 1 - x)
+        else:
+            part = outs[a].at[d, :, y if mine else 1 - y, :, at:at + n]
+            to = spot(d, z, 1 - y, x)
+        return send(part, part, bs.at[p], br.at[p], to)
+
+    def along_d(p, i, source):
+        a, at, n = pieces[p]
+        part = outs[a].at[source, :, :, :, at:at + n]
+        return send(part, part, ds.at[p, i - 1], dr.at[p, i - 1], spot(lax.rem(d + i, nd), z, y, x))
+
+    total = len(pieces)
+    for step in range(total + 3 * lag):
+        p = step
+        if p < total:
+            own(p).start()
+            for i in range(1, nz):
+                along_z(p, i, z).start()
+        p = step - lag
+        if 0 <= p < total:
+            own(p).wait()
+            for i in range(1, nz):
+                along_z(p, i, lax.rem(z - i + nz, nz)).wait_recv()
+            first_pair(p, True).start()
+        p = step - 2 * lag
+        if 0 <= p < total:
+            first_pair(p, False).wait_recv()
+            second_pair(p, True).start()
+        p = step - 3 * lag
+        if 0 <= p < total:
+            second_pair(p, False).wait_recv()
+            for i in range(1, nd):
+                along_d(p, i, d).start()
+    for p in range(total):
+        for i in range(1, nd):
+            along_d(p, i, lax.rem(d - i + nd, nd)).wait_recv()
+        for i in range(1, nz):
+            along_z(p, i, z).wait_send()
+        first_pair(p, True).wait_send()
+        second_pair(p, True).wait_send()
+        for i in range(1, nd):
+            along_d(p, i, d).wait_send()
+
+
+def gather_weights(nd, nt, shards, unit, lag=1, space=None):
+    nz = nt // 4
+    pieces = []
+    for a, s in enumerate(shards):
+        pieces += [(a, at, min(unit, s.shape[0])) for at in range(0, s.shape[0], unit)]
+    n = len(pieces)
+    dma = pltpu.SemaphoreType.DMA
+    outs = pl.pallas_call(
+        functools.partial(gather_body, nd, nz, pieces, lag, len(shards)),
+        out_shape=tuple(jax.ShapeDtypeStruct((nd, nz, 2, 2) + s.shape, s.dtype) for s in shards),
+        in_specs=[HBM] * len(shards),
+        out_specs=[space or HBM] * len(shards),
+        scratch_shapes=[dma((n,)), dma((n, nz - 1)), dma((n, nz - 1)), dma((n,)), dma((n,)), dma((n,)), dma((n,)),
+                        dma((n, nd - 1)), dma((n, nd - 1))],
+        compiler_params=pltpu.CompilerParams(collective_id=0, has_side_effects=True, vmem_limit_bytes=58 * 2**20),
+        name="gather_weights",
+    )(*shards)
+    return [o.reshape(nd, nt * s.shape[0], s.shape[1]) for o, s in zip(outs, shards)]
+
+
+def add_tiles(dst, src, tiles):
+    @pl.loop(0, tiles)
+    def _(i):
+        dst[i] = (dst[i].astype(jnp.float32) + src[i].astype(jnp.float32)).astype(dst.dtype)
+
+
+def scatter_body(nd, nz, chunks, rc, part, lag, ahead, count, *refs):
+    grads, vec = refs[:count], refs[count]
+    out, vout, own, sib, ra, rb, rz, vd, v1, vx, v2, vy, v3, vz, loc, ds, dr, as_, ar, bs, br, zs, zr, vs, vr = refs[count + 1:]
+    d, z, y, x = place(nd, nz)
+    meet(partners(nd, nz, d, z, y, x))
+    f32 = jnp.float32
+
+    def load(c):
+        a, at = chunks[c]
+        return pltpu.make_async_copy(grads[a].at[d, :, :, :, at:at + rc], own.at[c], loc.at[c])
+
+    def along_d(c, i):
+        a, at = chunks[c]
+        to = lax.rem(d + i, nd)
+        return send(grads[a].at[to, :, :, :, at:at + rc], sib.at[i - 1, c], ds.at[i - 1, c], dr.at[i - 1, c], spot(to, z, y, x))
+
+    def first_pair(c):
+        if c % 2 == 0:
+            return send(own.at[c, :, :, 1 - x], ra.at[c], as_.at[c], ar.at[c], spot(d, z, y, 1 - x))
+        return send(own.at[c, :, 1 - y], ra.at[c], as_.at[c], ar.at[c], spot(d, z, 1 - y, x))
+
+    def second_pair(c):
+        if c % 2 == 0:
+            return send(own.at[c, :, 1 - y, x], rb.at[c], bs.at[c], br.at[c], spot(d, z, 1 - y, x))
+        return send(own.at[c, :, y, 1 - x], rb.at[c], bs.at[c], br.at[c], spot(d, z, y, 1 - x))
+
+    def along_z(c, i):
+        to = lax.rem(z + i, nz)
+        return send(own.at[c, to, y, x], rz.at[i - 1, c], zs.at[i - 1, c], zr.at[i - 1, c], spot(d, to, y, x))
+
+    total = len(chunks)
+    top = vd.shape[1]
+
+    def vec_d(i):
+        to = lax.rem(d + i, nd)
+        return send(vec.at[:top], vd.at[d], vs.at[i - 1], vr.at[i - 1], spot(to, z, y, x))
+
+    def vec_x():
+        return send(v1, vx, vs.at[nd - 1], vr.at[nd - 1], spot(d, z, y, 1 - x))
+
+    def vec_y():
+        return send(v2, vy, vs.at[nd], vr.at[nd], spot(d, z, 1 - y, x))
+
+    def vec_z(i):
+        return send(v3, vz.at[z], vs.at[nd + i], vr.at[nd + i], spot(d, lax.rem(z + i, nz), y, x))
+
+    def vec_step(step):
+        if step == 0:
+            vd[d] = vec[:top]
+            for i in range(1, nd):
+                vec_d(i).start()
+        elif step == 1:
+            for i in range(1, nd):
+                vec_d(i).wait()
+            acc = vd[0]
+            for i in range(1, nd):
+                acc = acc + vd[i]
+            v1[:top] = acc
+            v1[top:] = vec[top:]
+            vec_x().start()
+        elif step == 2:
+            vec_x().wait()
+            v2[...] = v1[...] + vx[...]
+            vec_y().start()
+        elif step == 3:
+            vec_y().wait()
+            v3[...] = v2[...] + vy[...]
+            vz[z] = v3[...]
+            for i in range(1, nz):
+                vec_z(i).start()
+        elif step == 4:
+            for i in range(1, nz):
+                vec_z(i).wait()
+            acc = vz[0]
+            for i in range(1, nz):
+                acc = acc + vz[i]
+            vout[...] = acc
+
+    def begin(c):
+        load(c).start()
+        for i in range(1, nd):
+            along_d(c, i).start()
+
+    for c in range(min(ahead, total)):
+        begin(c)
+    for step in range(total + 3 * lag):
+        c = step
+        if c + ahead < total:
+            begin(c + ahead)
+        if step % 2 == 0:
+            vec_step(step // 2)
+        if c < total:
+            load(c).wait()
+            for i in range(1, nd):
+                along_d(c, i).wait_recv()
+
+            @pl.loop(0, nz)
+            def _(b):
+                for q in range(4):
+                    acc = own[c, b, q // 2, q % 2].astype(f32)
+                    for i in range(1, nd):
+                        acc = acc + sib[i - 1, c, b, q // 2, q % 2].astype(f32)
+                    own[c, b, q // 2, q % 2] = acc.astype(jnp.bfloat16)
+            first_pair(c).start()
+        c = step - lag
+        if 0 <= c < total:
+            first_pair(c).wait_recv()
+
+            @pl.loop(0, nz)
+            def _(b):
+                for q in range(2):
+                    at = (b, q, x) if c % 2 == 0 else (b, y, q)
+                    own[(c,) + at] = (own[(c,) + at].astype(f32) + ra[c, b, q].astype(f32)).astype(jnp.bfloat16)
+            second_pair(c).start()
+        c = step - 2 * lag
+        if 0 <= c < total:
+            second_pair(c).wait_recv()
+
+            @pl.loop(0, nz)
+            def _(b):
+                own[c, b, y, x] = (own[c, b, y, x].astype(f32) + rb[c, b].astype(f32)).astype(jnp.bfloat16)
+            for i in range(1, nz):
+                along_z(c, i).start()
+        c = step - 3 * lag
+        if 0 <= c < total:
+            for i in range(1, nz):
+                along_z(c, i).wait_recv()
+            acc = own[c, z, y, x].astype(f32)
+            for i in range(1, nz):
+                acc = acc + rz[i - 1, c].astype(f32)
+            out[c * rc:(c + 1) * rc] = acc
+    for c in range(total):
+        for i in range(1, nd):
+            along_d(c, i).wait_send()
+        first_pair(c).wait_send()
+        second_pair(c).wait_send()
+        for i in range(1, nz):
+            along_z(c, i).wait_send()
+
+
+def scatter_grads(nd, nt, grads, vec, top, rc, lag=2, ahead=3):
+    nz = nt // 4
+    part = grads[0].shape[2]
+    split = [g.reshape(nd, nz, 2, 2, g.shape[1] // nt, part) for g in grads]
+    chunks = []
+    for a, g in enumerate(split):
+        chunks += [(a, at) for at in range(0, g.shape[4], rc)]
+    n = len(chunks)
+    dma = pltpu.SemaphoreType.DMA
+    bf = jnp.bfloat16
+    wide = vec.shape[1]
+
+    def vv(shape):
+        return pltpu.VMEM(shape, jnp.float32)
+
+    return pl.pallas_call(
+        functools.partial(scatter_body, nd, nz, chunks, rc, part, lag, ahead, len(grads)),
+        out_shape=(jax.ShapeDtypeStruct((n * rc, part), jnp.float32), jax.ShapeDtypeStruct(vec.shape, vec.dtype)),
+        in_specs=[HBM] * len(grads) + [VMEM],
+        out_specs=[VMEM, VMEM],
+        scratch_shapes=[pltpu.VMEM((n, nz, 2, 2, rc, part), bf), pltpu.VMEM((nd - 1, n, nz, 2, 2, rc, part), bf),
+                        pltpu.VMEM((n, nz, 2, rc, part), bf), pltpu.VMEM((n, nz, rc, part), bf), pltpu.VMEM((nz - 1, n, rc, part), bf),
+                        vv((nd, top, wide)), vv(vec.shape), vv(vec.shape), vv(vec.shape), vv(vec.shape), vv(vec.shape), vv((nz,) + vec.shape),
+                        dma((n,)), dma((nd - 1, n)), dma((nd - 1, n)), dma((n,)), dma((n,)), dma((n,)), dma((n,)),
+                        dma((nz - 1, n)), dma((nz - 1, n)), dma((nd + nz,)), dma((nd + nz,))],
+        compiler_params=pltpu.CompilerParams(collective_id=1, has_side_effects=True, vmem_limit_bytes=58 * 2**20),
+        name="scatter_grads",
+    )(*split, vec)
+
+
 def local(nd, nt, x, num, den, top, prev_a, prev_f, n1g, n1b, fading, reward, mk, mv, mr, wk, wv, wr, wo, n2g, n2b, ck, cr,
           fk, fv, fr, up):
     rows, dim = x.shape
@@ -282,12 +582,8 @@
     ahead = [(i, i + 1) for i in range(nt - 1)]
     behind = [(i + 1, i) for i in range(nt - 1)]
 
-    def gather(shard):
-        whole = lax.all_gather(shard.T, ("dp", "tensor"), axis=0, tiled=True)
-        return whole.reshape(nd, nt * shard.shape[1], shard.shape[0])
-
-    whole_k, whole_v, whole_r, whole_o = gather(wk), gather(wv), gather(wr), gather(wo)
-    whole_fk, whole_fv, whole_fr = gather(fk), gather(fv), gather(fr)
+    whole_k, whole_v, whole_r, whole_o, whole_fk, whole_fv, whole_fr = gather_weights(
+        nd, nt, [s.T for s in (wk, wv, wr, wo, fk, fv, fr)], 32, 2)
     states = lax.all_gather(jnp.stack([num, den, top]), "tensor", axis=2, tiled=True)
 
     def into(left, whole):
@@ -414,22 +710,20 @@
     g_tok, grad_g1, grad_b1 = norm_back(g_first, s1, scale1, n1g)
     tokens_grad = g_middle + g_tok
 
-    def scatter(stack):
-        cols = stack.shape[1]
-        mine = lax.psum_scatter(stack.reshape(nd * cols, part), "dp", scatter_dimension=0, tiled=True)
-        mine = lax.psum_scatter(mine, "tensor", scatter_dimension=0, tiled=True)
-        return mine.astype(jnp.float32).T
-
-    out_k, out_v, out_r, out_o = scatter(grad_k), scatter(grad_v), scatter(grad_r), scatter(grad_o)
-    out_fk, out_fv, out_fr = scatter(grad_fk), scatter(grad_fv), scatter(grad_fr)
-
     vectors = jnp.stack([grad_g1, grad_b1, gw[0] * w, gu[0], grad_mk, grad_mv, grad_mr, grad_g2, grad_b2, grad_ck, grad_cr])
     lead = jnp.where(pos == 0, 1.0, 0.0)
-    slots = jnp.zeros((2, nd, seqs, dim), jnp.float32)
-    pair = (jnp.stack([back1[0], back2[0]]) * lead)[:, None, None, :]
-    slots = lax.dynamic_update_slice(slots, pair, (0, dp, seq, 0))
-    vectors, slots = lax.psum((vectors, slots), ("dp", "tensor"))
-    prevs = lax.dynamic_index_in_dim(slots, dp, axis=1, keepdims=False)
+    pair = (jnp.stack([back1[0], back2[0]]) * lead)[:, None, :]
+    slots = lax.dynamic_update_slice(jnp.zeros((2, seqs, dim), jnp.float32), pair, (0, seq, 0)).reshape(2 * seqs, dim)
+    tail_rows = -(-2 * seqs // 8) * 8
+    vec = jnp.concatenate([vectors, jnp.zeros((5, dim), jnp.float32), slots, jnp.zeros((tail_rows - 2 * seqs, dim), jnp.float32)])
+    unit = sum(s.shape[1] for s in (wk, wv, wr, wo, fk, fv, fr)) // 26
+    summed, vectors = scatter_grads(nd, nt, [grad_k, grad_v, grad_r, grad_o, grad_fk, grad_fv, grad_fr], vec, 16, unit)
+    prevs = vectors[16:16 + 2 * seqs].reshape(2, seqs, dim)
+    outs, at = [], 0
+    for s in (wk, wv, wr, wo, fk, fv, fr):
+        outs.append(summed[at:at + s.shape[1]].T)
+        at += s.shape[1]
+    out_k, out_v, out_r, out_o, out_fk, out_fv, out_fr = outs
     return (result, tokens_grad, grad_num, grad_den, grad_top, prevs[0], prevs[1],
             vectors[0], vectors[1], vectors[2], vectors[3], vectors[4], vectors[5], vectors[6],
             out_k, out_v, out_r, out_o, vectors[7], vectors[8], vectors[9], vectors[10], out_fk, out_fv, out_fr)

time: 1390 us -> 567 us (0.41)
  waiting for transfers between devices: 1020 us -> 1.26 us
  Pallas kernels: 10.8 us -> 274 us
  matrix products: 77.7 us -> 37.1 us
    reduce_scatter x14 -> x0, waiting for transfers between devices: 565 us -> none  [the longest x7 565 us: scatter(): mine = lax.psum_scatter(mine, 'tensor', scatter_dimension=0, tiled=True)]
    all_gather x7 -> x0, waiting for transfers between devices: 320 us -> none  [gather(): whole = lax.all_gather(shard.T, ('dp', 'tensor'), axis=0, tiled=True)]
    pallas_call x0 -> x2, Pallas kernels: none -> 263 us  [the longest x1 133 us: scatter_grads(): pl.pallas_call(functools.partial(scatter_body, nd, nz, chunks, rc, part,...]
    psum x1 -> x0, waiting for transfers between devices: 117 us -> none  [local(): vectors, slots = lax.psum((vectors, slots), ('dp', 'tensor'))]
    slice x0 -> x12, local copies, waits for them, and re-layouts: none -> 34 us  [the longest x1 12.5 us: outof(): return jnp.concatenate([dot_nn(left, whole[d]) for d in range(nd)], axis=1)]
    reshape x2 -> x1, local copies, waits for them, and re-layouts: 23 us -> 0.02 us  [local(): lax.dynamic_update_slice(jnp.zeros((2, seqs, dim), jnp.float32), pair, (0...]
    dot_general x14, matrix products: 36.8 us -> 15 us  [dot_nt(): lax.dot_general(x, y, (((1,), (1,)), ((), ())), preferred_element_type=jn...]
    dot_general x14, matrix products: 27.6 us -> 10.2 us  [dot_nn(): lax.dot_general(x, y, (((1,), (0,)), ((), ())), preferred_element_type=jn...]
  transfers between devices with their start and end apart: 26 -> 4, of which waited for: 17 -> 1; matrix products, arithmetic and copies ran while one was open for 12% -> 13% of each run, Pallas kernels for 1% -> 23%
where the time goes in v2:
time: 567 us; the launch traced here: 563 us
  Pallas kernels  274 us (48%)
  blocking collectives  126 us (22%)
  local copies, waits for them, and re-layouts  67.6 us (12%)
  other arithmetic  42.9 us (8%)
  matrix products  37.1 us (7%)
  starting transfers between devices  11.3 us (2%)
    pallas_call x1, Pallas kernels, scatter_grads(): pl.pallas_call(functools.partial(scatter_body, nd, nz, chunks, rc, part,...  133 us
    pallas_call x1, Pallas kernels, gather_weights(): pl.pallas_call(functools.partial(gather_body, nd, nz, pieces, lag, len(sh...  131 us
    all_gather x2, blocking collectives, local(): got = lax.all_gather(sent, 'tensor', axis=0)  77.5 us
    all_gather x1, blocking collectives, local(): lax.all_gather(jnp.stack([num, den, top]), 'tensor', axis=2, tiled=True)  48.2 us
    another operation x7, other arithmetic, weight_grad(): return jnp.stack([both[:, d * part:(d + 1) * part] for d in range(nd)])  24.4 us
    dot_general x14, matrix products, dot_nt(): lax.dot_general(x, y, (((1,), (1,)), ((), ())), preferred_element_type=jn...  15 us
    unnamed x190, local copies, waits for them, and re-layouts  12.9 us
    slice x1, local copies, waits for them, and re-layouts, outof(): return jnp.concatenate([dot_nn(left, whole[d]) for d in range(nd)], axis=1)  12.5 us
  transfers between devices with their start and end apart: 4, of which 1 were waited for; matrix products, arithmetic and copies ran while one was open for 13% of the time, Pallas kernels for 23%

profile of v2, /device:TPU:0, one launch (start us, length us, event | category | flops | bytes accessed | tf_op | source)
XLA Modules:
  0.0 562.8 jit_solution(10166946067946107040)
XLA Ops:
  0.7 1.4 reduce_sum.171
  2.1 1.5 multiply_reduce_fusion.11
  3.6 1.5 add_convert_fusion.1
  5.9 4.8 collective-permute-start
  10.8 1.8 copy.59
  13.4 130.8 %gather_weights.1 = (bf16[2,4,2,2,64,512]{5,4,3,2,1,0:T(8,128)(2,1)}, bf16[2,4,2,2,64,512]{5,4,3,2,1,0:T(8,128)(2,1)}, bf16[2,4,2,2,64,512]{5,4,3,2,1,0:T(8,128)...) custom-call(bf16[64,512]{1,0:T(8,128)(2,1)} %bitcast.427, ...), custom_call_target="tpu_custom_call" | custom-call | tf_op jit(solution)/shard_map/gather_weights/pallas_call | solution.py:382
  144.2 1.7 fusion.155
  146.2 48.2 %all_gather.15 = f32[3,2,1024]{0,1,2:T(2,128)} all-gather(f32[3,2,64]{0,1,2:T(2,128)S(1)} %copy.61), channel_id=1, replica_groups=mesh['dp'=2,'tensor'=16] {'tensor'}, dimensions={2}, use_global_device_ids=true | all-gather | bytes 26112 | tf_op jit(solution)/shard_map/all_gather | solution.py:587
  194.4 12.5 %fusion.144 = (bf16[1,4,2,2,256,512]{5,4,3,2,1,0:T(8,128)(2,1)}, bf16[1,4,2,2,256,512]{5,4,3,2,1,0:T(8,128)(2,1)}, bf16[1,4,2,2,256,512]{5,4,3,2,1,0:T(8,128)(2,1)}, bf16[1,4,2,2,256,512]{5,4,3,2,1,0:T(8,128)(2,1)}) fusion(bf16[2,4,2,2,256,512]{5,4,3,2,1,0:T(8,128)(2,1)} %get-tuple-element.60, bf16[2,4,2,2,256,512]{5,4,3,2,1,0:T(8,128)(2,1)} %get-tuple-element.59), kind=kLoop, calls=%fused_computation.389 | loop fusion | bytes 33554432 | tf_op jit(solution)/shard_map/slice | solution.py:596
  206.9 4.5 fusion.153
  211.4 2.1 fusion.151
  213.6 11.0 %dynamic-slice_reduce_fusion = (f32[1024]{0:T(1024)S(1)}, f32[1024]{0:T(1024)S(1)}, f32[1024]{0:T(1024)S(1)}) fusion(f32[3,2,1024]{0,1,2:T(2,128)S(1)} %copy-done.37, s32[]{:T(128)S(6)} %add.802, s32[]{:T(128)S(6)} %select_n.354, s32[]{:T(128)S(6)} %add.782), kind=kLoop, calls=%fused_computation.90 | loop fusion | bytes 24588 | tf_op jit(solution)/shard_map/slice | solution.py:628
  224.7 2.0 fusion.17
  229.6 36.9 %all-gather.2 = f32[16,3,1024]{2,1,0:T(4,128)S(1)} all-gather(f32[1,3,1024]{2,1,0:T(4,128)S(1)} %maximum_bitcast_fusion), channel_id=2, replica_groups=mesh['dp'=2,'tensor'=16] {'tensor'}, dimensions={0}, use_global_device_ids=true | all-gather | bytes 208896 | tf_op jit(solution)/shard_map/all_gather | solution.py:625
  267.8 3.4 wkv_forward.1
  274.2 3.8 collective-permute-start.1
  279.4 1.9 fusion.11
  281.3 3.7 fusion.27
  291.6 1.8 multiply_convert_fusion.2
  296.3 2.2 fusion.3
  298.6 1.3 fusion.161
  302.1 5.7 %convolution_convert_fusion.1 = bf16[4096,1024]{1,0:T(8,128)(2,1)} fusion(bf16[256,4096]{1,0:T(8,128)(2,1)S(1)} %fusion.3, bf16[256,1024]{1,0:T(8,128)(2,1)S(1)} %get-tuple-element.226), kind=kOutput, calls=%fused_computation.3 | convolution fusion | flops 2151677952 | bytes 11010048 | tf_op jit(solution)/shard_map/dot_general | solution.py:40
  307.8 2.6 convolution_convert_fusion
  313.2 5.8 %fusion.143 = (bf16[4096,512]{1,0:T(8,128)(2,1)}, bf16[4096,512]{1,0:T(8,128)(2,1)}) fusion(bf16[4096,1024]{1,0:T(8,128)(2,1)} %convolution_convert_fusion.1), kind=kLoop, calls=%fused_computation.388 | loop fusion | bytes 16777216 | tf_op jit(solution)/shard_map/slice | solution.py:600
  319.0 3.9 fusion.142
  322.8 1.5 fusion.146
  324.3 7.5 %pad_maximum_fusion.refs_4_ = bf16[2,4,2,2,256,512]{5,4,3,2,1,0:T(8,128)(2,1)} fusion(bf16[1,4,2,2,256,512]{5,4,3,2,1,0:T(8,128)(2,1)} %bitcast.365, bf16[1,4,2,2,256,512]{5,4,3,2,1,0:T(8,128)(2,1)} %bitcast.364), kind=kLoop, calls=%fused_computation | loop fusion | flops 4194304 | bytes 16777216 | tf_op jit(solution)/shard_map/stack | solution.py:600
  331.8 7.5 %pad_maximum_fusion.1.refs_5_ = bf16[2,4,2,2,256,512]{5,4,3,2,1,0:T(8,128)(2,1)} fusion(bf16[1,4,2,2,256,512]{5,4,3,2,1,0:T(8,128)(2,1)} %bitcast.367, bf16[1,4,2,2,256,512]{5,4,3,2,1,0:T(8,128)(2,1)} %bitcast.366), kind=kLoop, calls=%fused_computation.1 | loop fusion | flops 4194304 | bytes 16777216 | tf_op jit(solution)/shard_map/stack | solution.py:600
  339.4 3.2 pad_maximum_fusion.6.refs_6_
  343.8 1.4 fusion.140
  346.2 2.4 wkv_carry.1
  348.7 40.6 %all-gather.3 = f32[16,3,1024]{2,1,0:T(4,128)S(1)} all-gather(f32[1,3,1024]{2,1,0:T(4,128)S(1)} %maximum_bitcast_fusion.1), channel_id=3, replica_groups=mesh['dp'=2,'tensor'=16] {'tensor'}, dimensions={0}, use_global_device_ids=true | all-gather | bytes 208896 | tf_op jit(solution)/shard_map/all_gather | solution.py:674
  389.4 4.9 wkv_backward.1
  401.5 1.3 collective-permute-start.3
  403.4 1.5 pad_maximum_fusion.2.refs_0_
  404.9 1.5 pad_maximum_fusion.3.refs_1_
  406.4 1.6 pad_maximum_fusion.4.refs_2_
  408.0 1.5 pad_maximum_fusion.5.refs_3_
  411.8 3.2 multiply_reduce_fusion.6
  415.0 1.9 concatenate.65.refs_7_
  416.9 132.7 %scatter_grads.1 = (f32[832,512]{1,0:T(8,128)}, f32[24,1024]{1,0:T(8,128)}) custom-call(bf16[2,4,2,2,64,512]{5,4,3,2,1,0:T(8,128)(2,1)} %pad_maximum_fusion.2.refs_0_, bf16[2,4,2,2,64,512]{5,4,3,2,1,0:T(8,128)(2,1)} %pad_maximum_fusion.3.refs_1_, bf16[2,4,2,2,64,512]{5,4,3,2,1,0:T(8,128)(2,1)} %pad_maximum_fusion.4.refs_2_, ...), custom_call_target="tpu_custom_call" | custom-call | tf_op jit(solution)/shard_map/scatter_grads/pallas_call | solution.py:556
  549.7 1.5 fusion.157
  551.2 1.7 fusion.156
  552.9 2.0 slice_bitcast_fusion.2
  554.9 2.2 slice_bitcast_fusion
  557.1 2.0 copy.62
  559.2 2.0 copy.63
  561.2 1.4 multiply_add_fusion
  (273 shorter events, 36.2 us)
Async XLA Ops:
  0.7 11.9 %copy-start.77 = (bf16[512,256]{1,0:T(8,128)(2,1)S(1)}, bf16[512,256]{1,0:T(8,128)(2,1)}, u32[]{:S(2)}) copy-start(bf16[512,256]{1,0:T(8,128)(2,1)} %param.47) | copy-start | bytes 786436
  2.1 143.9 %copy-start.83 = (f32[1024]{0:T(1024)S(1)}, f32[1024]{0:T(1024)}, u32[]{:S(2)}) copy-start(f32[1024]{0:T(1024)} %param.35) | copy-start | bytes 12292
  2.1 143.9 %copy-start.90 = (f32[2,64]{1,0:T(2,128)S(1)}, f32[2,64]{1,0:T(2,128)}, u32[]{:S(2)}) copy-start(f32[2,64]{1,0:T(2,128)} %param.27) | copy-start | bytes 1540
  2.1 143.9 %copy-start.91 = (f32[2,64]{1,0:T(2,128)S(1)}, f32[2,64]{1,0:T(2,128)}, u32[]{:S(2)}) copy-start(f32[2,64]{1,0:T(2,128)} %param.26) | copy-start | bytes 1540
  2.1 143.9 %copy-start.92 = (f32[2,64]{1,0:T(2,128)S(1)}, f32[2,64]{1,0:T(2,128)}, u32[]{:S(2)}) copy-start(f32[2,64]{1,0:T(2,128)} %param.28) | copy-start | bytes 1540
  5.9 218.7 %collective-permute-start = (bf16[1,1024]{1,0:T(2,128)(2,1)S(1)}, bf16[1,1024]{1,0:T(2,128)(2,1)S(1)}, u32[]{:S(2)}, u32[]{:S(2)}) collective-permute-start(bf16[1,1024]{1,0:T(2,128)(2,1)S(1)} %slice.709), channel_id=1, source_target_pairs={{0,1},{1,2},{2,3},{3,4},{4,5},{5,6},{6,7},{7,8},{8,9},{9,10},{10,1... | collective-permute-start | bytes 6152 | tf_op jit(solution)/shard_map/ppermute | solution.py:603
  145.9 80.9 %copy-start.20 = (bf16[1,4,2,2,64,512]{5,4,3,2,1,0:T(8,128)(2,1)}, bf16[1,4,2,2,64,512]{5,4,3,2,1,0:T(8,128)(2,1)S(1)}, u32[]{:S(2)}) copy-start(bf16[1,4,2,2,64,512]{5,4,3,2,1,0:T(8,128)(2,1)S(1)} %get-tuple-element.218) | copy-start | bytes 3145732
  146.0 81.8 %copy-start.22 = (bf16[1,4,2,2,64,512]{5,4,3,2,1,0:T(8,128)(2,1)}, bf16[1,4,2,2,64,512]{5,4,3,2,1,0:T(8,128)(2,1)S(1)}, u32[]{:S(2)}) copy-start(bf16[1,4,2,2,64,512]{5,4,3,2,1,0:T(8,128)(2,1)S(1)} %get-tuple-element.217) | copy-start | bytes 3145732
  194.3 12.5 %copy-start.84 = (f32[1024]{0:T(1024)S(1)}, f32[1024]{0:T(1024)}, u32[]{:S(2)}) copy-start(f32[1024]{0:T(1024)} %param.37) | copy-start | bytes 12292
  194.4 12.5 %copy-start.85 = (f32[1024]{0:T(1024)S(1)}, f32[1024]{0:T(1024)}, u32[]{:S(2)}) copy-start(f32[1024]{0:T(1024)} %param.36) | copy-start | bytes 12292
  206.9 4.5 copy-start.73
  206.9 4.5 copy-start.74
  211.4 13.3 %copy-start.78 = (f32[1024]{0:T(1024)S(1)}, f32[1024]{0:T(1024)}, u32[]{:S(2)}) copy-start(f32[1024]{0:T(1024)} %param.33) | copy-start | bytes 12292
  211.4 13.3 %copy-start.88 = (bf16[2,1024]{1,0:T(2,128)(2,1)S(1)}, bf16[2,1024]{1,0:T(2,128)(2,1)}, u32[]{:S(2)}) copy-start(bf16[2,1024]{1,0:T(2,128)(2,1)} %param.29) | copy-start | bytes 12292
  211.4 13.3 %copy-start.11 = (f32[256,1024]{1,0:T(8,128)S(1)}, f32[256,1024]{1,0:T(8,128)}, u32[]{:S(2)}) copy-start(f32[256,1024]{1,0:T(8,128)} %param.25) | copy-start | bytes 3145732
  211.4 13.3 %copy-start.80 = (f32[1024]{0:T(1024)S(1)}, f32[1024]{0:T(1024)}, u32[]{:S(2)}) copy-start(f32[1024]{0:T(1024)} %param.31) | copy-start | bytes 12292
  211.4 13.3 %copy-start.82 = (f32[1024]{0:T(1024)S(1)}, f32[1024]{0:T(1024)}, u32[]{:S(2)}) copy-start(f32[1024]{0:T(1024)} %param.32) | copy-start | bytes 12292
  226.8 40.2 %copy-start.56 = (bf16[256,1024]{1,0:T(8,128)(2,1)}, bf16[256,1024]{1,0:T(8,128)(2,1)S(1)}, u32[]{:S(2)}) copy-start(bf16[256,1024]{1,0:T(8,128)(2,1)S(1)} %get-tuple-element.228) | copy-start | bytes 1572868
  227.8 38.8 %copy-start.28 = (bf16[1,4,2,2,64,512]{5,4,3,2,1,0:T(8,128)(2,1)S(1)}, bf16[1,4,2,2,64,512]{5,4,3,2,1,0:T(8,128)(2,1)}, u32[]{:S(2)}) copy-start(bf16[1,4,2,2,64,512]{5,4,3,2,1,0:T(8,128)(2,1)} %get-tuple-element.214) | copy-start | bytes 3145732
  228.3 38.7 %copy-start.30 = (bf16[1,4,2,2,64,512]{5,4,3,2,1,0:T(8,128)(2,1)S(1)}, bf16[1,4,2,2,64,512]{5,4,3,2,1,0:T(8,128)(2,1)}, u32[]{:S(2)}) copy-start(bf16[1,4,2,2,64,512]{5,4,3,2,1,0:T(8,128)(2,1)} %get-tuple-element.213) | copy-start | bytes 3145732
  229.6 38.2 %copy-start.10 = (f32[1024]{0:T(1024)S(1)}, f32[1024]{0:T(1024)}, u32[]{:S(2)}) copy-start(f32[1024]{0:T(1024)} %param.34) | copy-start | bytes 12292
  267.0 4.3 copy-start.32
  267.1 4.8 copy-start.34
  267.5 4.7 copy-start.12
  271.8 6.3 %copy-start.86 = (f32[1024]{0:T(1024)S(1)}, f32[1024]{0:T(1024)}, u32[]{:S(2)}) copy-start(f32[1024]{0:T(1024)} %param.44) | copy-start | bytes 12292
  271.8 6.3 %copy-start.87 = (f32[1024]{0:T(1024)S(1)}, f32[1024]{0:T(1024)}, u32[]{:S(2)}) copy-start(f32[1024]{0:T(1024)} %param.45) | copy-start | bytes 12292
  271.8 7.6 %copy-start.89 = (bf16[2,1024]{1,0:T(2,128)(2,1)S(1)}, bf16[2,1024]{1,0:T(2,128)(2,1)}, u32[]{:S(2)}) copy-start(bf16[2,1024]{1,0:T(2,128)(2,1)} %param.30) | copy-start | bytes 12292
  274.2 5.2 collective-permute-start.1
  281.3 9.9 %copy-start.65 = (bf16[256,1024]{1,0:T(8,128)(2,1)}, bf16[256,1024]{1,0:T(8,128)(2,1)S(1)}, u32[]{:S(2)}) copy-start(bf16[256,1024]{1,0:T(8,128)(2,1)S(1)} %get-tuple-element.227) | copy-start | bytes 1572868
  293.8 17.4 %copy-start.48 = (f32[256,512]{1,0:T(8,128)}, f32[256,512]{1,0:T(8,128)S(1)}, u32[]{:S(2)}) copy-start(f32[256,512]{1,0:T(8,128)S(1)} %fusion.163) | copy-start | bytes 1572868
  300.8 10.4 %copy-start.69 = (f32[256,512]{1,0:T(8,128)}, f32[256,512]{1,0:T(8,128)S(1)}, u32[]{:S(2)}) copy-start(f32[256,512]{1,0:T(8,128)S(1)} %fusion.161) | copy-start | bytes 1572868
  302.1 9.1 %copy-start.71 = (f32[256,512]{1,0:T(8,128)}, f32[256,512]{1,0:T(8,128)S(1)}, u32[]{:S(2)}) copy-start(f32[256,512]{1,0:T(8,128)S(1)} %fusion.160) | copy-start | bytes 1572868
  302.1 5.7 %copy-start.68 = (bf16[256,1024]{1,0:T(8,128)(2,1)S(1)}, bf16[256,1024]{1,0:T(8,128)(2,1)}, u32[]{:S(2)}) copy-start(bf16[256,1024]{1,0:T(8,128)(2,1)} %copy-done.67) | copy-start | bytes 1572868
  311.8 7.1 %copy-start.60 = (f32[256,1024]{1,0:T(8,128)}, f32[256,1024]{1,0:T(8,128)S(1)}, u32[]{:S(2)}) copy-start(f32[256,1024]{1,0:T(8,128)S(1)} %get-tuple-element.195) | copy-start | bytes 3145732
  311.9 30.8 %collective-permute-start.2 = (f32[1,1024]{1,0:T(1,128)S(1)}, f32[1,1024]{1,0:T(1,128)S(1)}, u32[]{:S(2)}, u32[]{:S(2)}) collective-permute-start(f32[1,1024]{1,0:T(1,128)S(1)} %get-tuple-element.234), channel_id=1, source_target_pairs={{1,0},{2,1},{3,2},{4,3},{5,4},{6,5},{7,6},{8,7},{9,8},{10,9},{11,1... | collective-permute-start | bytes 12296 | tf_op jit(solution)/shard_map/ppermute | solution.py:609
  346.2 43.2 %copy-start.7 = (f32[8,256,128]{2,1,0:T(8,128)S(1)}, f32[8,256,128]{2,1,0:T(8,128)}, u32[]{:S(2)}) copy-start(f32[8,256,128]{2,1,0:T(8,128)} %copy-done.6) | copy-start | bytes 3145732
  346.2 43.2 %copy-start.9 = (f32[8,256,128]{2,1,0:T(8,128)S(1)}, f32[8,256,128]{2,1,0:T(8,128)}, u32[]{:S(2)}) copy-start(f32[8,256,128]{2,1,0:T(8,128)} %copy-done.8) | copy-start | bytes 3145732
  389.4 4.9 copy-start.31
  389.4 5.4 copy-start.29
  395.2 5.2 copy-start.40
  396.0 4.5 copy-start.42
  396.4 4.0 copy-start.44
  401.5 10.3 %collective-permute-start.3 = (f32[1,1024]{1,0:T(1,128)S(1)}, f32[1,1024]{1,0:T(1,128)S(1)}, u32[]{:S(2)}, u32[]{:S(2)}) collective-permute-start(f32[1,1024]{1,0:T(1,128)S(1)} %get-tuple-element.232), channel_id=1, source_target_pairs={{1,0},{2,1},{3,2},{4,3},{5,4},{6,5},{7,6},{8,7},{9,8},{10,9},{11,1... | collective-permute-start | bytes 12296 | tf_op jit(solution)/shard_map/ppermute | solution.py:609
  408.0 3.8 copy-start.41
  408.0 3.8 copy-start.43
  408.0 3.8 copy-start.45
  549.6 11.6 %copy-start.62 = (f32[256,1024]{1,0:T(8,128)S(1)}, f32[256,1024]{1,0:T(8,128)}, u32[]{:S(2)}) copy-start(f32[256,1024]{1,0:T(8,128)} %get-tuple-element.182) | copy-start | bytes 3145732
  549.6 11.6 %copy-start.63 = (f32[256,1024]{1,0:T(8,128)S(1)}, f32[256,1024]{1,0:T(8,128)}, u32[]{:S(2)}) copy-start(f32[256,1024]{1,0:T(8,128)} %get-tuple-element.180) | copy-start | bytes 3145732
  (49 other events, 110.1 us)

commit v3 on v2

--- a/solution.py
+++ b/solution.py
@@ -52,90 +52,6 @@
 
 def lane(c):
     return slice(c * LANES, (c + 1) * LANES)
-
-
-def wkv_forward_body(k_ref, v_ref, r_ref, w_ref, u_ref, a0_ref, b0_ref, m0_ref,
-                     g_ref, kb, vb, yb, mb, ab, bb, sm, sa, sb):
-    rows, width = k_ref.shape
-    chunks = rows // STEP
-    for c in range(width // LANES):
-        kb[c] = k_ref[:, lane(c)]
-        vb[c] = v_ref[:, lane(c)]
-
-    for group in scan_groups(width):
-        m = [jnp.full((chunks, LANES), NEG, jnp.float32) for _ in group]
-        a = [jnp.zeros((chunks, LANES), jnp.float32) for _ in group]
-        b = [jnp.zeros((chunks, LANES), jnp.float32) for _ in group]
-        for j in range(STEP):
-            at = pl.ds(j, chunks, stride=STEP)
-            for i, c in enumerate(group):
-                k = kb[c, at, :]
-                mw = m[i] - w_ref[:, lane(c)]
-                m[i] = jnp.maximum(mw, k)
-                keep = jnp.exp(mw - m[i])
-                take = jnp.exp(k - m[i])
-                a[i] = keep * a[i] + take * vb[c, at, :]
-                b[i] = keep * b[i] + take
-        for i, c in enumerate(group):
-            sm[:, lane(c)] = m[i]
-            sa[:, lane(c)] = a[i]
-            sb[:, lane(c)] = b[i]
-
-    w = w_ref[...]
-    m, a, b = m0_ref[...], a0_ref[...], b0_ref[...]
-    for s in range(chunks):
-        me, ae, be = sm[s:s + 1, :], sa[s:s + 1, :], sb[s:s + 1, :]
-        sm[s:s + 1, :] = m
-        sa[s:s + 1, :] = a
-        sb[s:s + 1, :] = b
-        mw = m - float(STEP) * w
-        m = jnp.maximum(mw, me)
-        keep = jnp.exp(mw - m)
-        take = jnp.exp(me - m)
-        a = keep * a + take * ae
-        b = keep * b + take * be
-
-    for group in scan_groups(width):
-        m = [sm[:, lane(c)] for c in group]
-        a = [sa[:, lane(c)] for c in group]
-        b = [sb[:, lane(c)] for c in group]
-        for j in range(STEP):
-            at = pl.ds(j, chunks, stride=STEP)
-            for i, c in enumerate(group):
-                k = kb[c, at, :]
-                v = vb[c, at, :]
-                mb[c, at, :] = m[i]
-                ab[c, at, :] = a[i]
-                bb[c, at, :] = b[i]
-                uk = u_ref[:, lane(c)] + k
-                p = jnp.maximum(m[i], uk)
-                alpha = jnp.exp(m[i] - p)
-                beta = jnp.exp(uk - p)
-                yb[c, at, :] = (alpha * a[i] + beta * v) / (alpha * b[i] + beta)
-                mw = m[i] - w_ref[:, lane(c)]
-                m[i] = jnp.maximum(mw, k)
-                keep = jnp.exp(mw - m[i])
-                take = jnp.exp(k - m[i])
-                a[i] = keep * a[i] + take * v
-                b[i] = keep * b[i] + take
-    for c in range(width // LANES):
-        g_ref[:, lane(c)] = (jax.nn.sigmoid(r_ref[:, lane(c)]) * yb[c]).astype(jnp.bfloat16)
-
-
-def wkv_forward(k, v, r, w, u, a0, b0, m0):
-    rows, width = k.shape
-    block = jax.ShapeDtypeStruct((width // LANES, rows, LANES), jnp.float32)
-    chunks = rows // STEP
-    return pl.pallas_call(
-        wkv_forward_body,
-        out_shape=(jax.ShapeDtypeStruct((rows, width), jnp.bfloat16),) + (block,) * 6,
-        in_specs=[VMEM] * 8,
-        out_specs=[VMEM] * 7,
-        scratch_shapes=[pltpu.VMEM((chunks, width), jnp.float32)] * 3,
-        compiler_params=pltpu.CompilerParams(vmem_limit_bytes=40 * 2**20),
-        cost_estimate=pl.CostEstimate(flops=60 * rows * width, transcendentals=7 * rows * width, bytes_accessed=36 * rows * width),
-        name="wkv_forward",
-    )(k, v, r, w, u, a0, b0, m0)
 
 
 def wkv_carry_body(r_ref, gg_ref, kb, yb, mb, bb, w_ref, u_ref, gyb, ca_ref, cb_ref, lc_ref, la_ref, lb_ref, lg_ref):
@@ -299,11 +215,104 @@
     return pltpu.make_async_remote_copy(src_ref=src, dst_ref=dst, send_sem=send_sem, recv_sem=recv_sem, device_id=to, device_id_type=MESH)
 
 
-def gather_body(nd, nz, pieces, lag, count, *refs):
-    ins, outs = refs[:count], refs[count:2 * count]
-    loc, zs, zr, as_, ar, bs, br, ds, dr = refs[2 * count:]
+def rowwise_norm(x):
+    center = x - jnp.mean(x, axis=-1, keepdims=True)
+    return center * lax.rsqrt(jnp.mean(center * center, axis=-1, keepdims=True) + EPS)
+
+
+def scan_ends(kb, vb, w_ref, sm, sa, sb, width, chunks):
+    for group in scan_groups(width):
+        m = [jnp.full((chunks, LANES), NEG, jnp.float32) for _ in group]
+        a = [jnp.zeros((chunks, LANES), jnp.float32) for _ in group]
+        b = [jnp.zeros((chunks, LANES), jnp.float32) for _ in group]
+        for j in range(STEP):
+            at = pl.ds(j, chunks, stride=STEP)
+            for i, c in enumerate(group):
+                k = kb[c, at, :]
+                mw = m[i] - w_ref[:, lane(c)]
+                m[i] = jnp.maximum(mw, k)
+                keep = jnp.exp(mw - m[i])
+                take = jnp.exp(k - m[i])
+                a[i] = keep * a[i] + take * vb[c, at, :]
+                b[i] = keep * b[i] + take
+        for i, c in enumerate(group):
+            sm[:, lane(c)] = m[i]
+            sa[:, lane(c)] = a[i]
+            sb[:, lane(c)] = b[i]
+
+
+def join(m, a, b, decay, me, ae, be):
+    mw = m - decay
+    mn = jnp.maximum(mw, me)
+    keep = jnp.exp(mw - mn)
+    take = jnp.exp(me - mn)
+    return mn, keep * a + take * ae, keep * b + take * be
+
+
+def scan_rows(kb, vb, yb, mb, ab, bb, w_ref, u_ref, sm, sa, sb, width, chunks):
+    for group in scan_groups(width):
+        m = [sm[:, lane(c)] for c in group]
+        a = [sa[:, lane(c)] for c in group]
+        b = [sb[:, lane(c)] for c in group]
+        for j in range(STEP):
+            at = pl.ds(j, chunks, stride=STEP)
+            for i, c in enumerate(group):
+                k = kb[c, at, :]
+                v = vb[c, at, :]
+                mb[c, at, :] = m[i]
+                ab[c, at, :] = a[i]
+                bb[c, at, :] = b[i]
+                uk = u_ref[:, lane(c)] + k
+                p = jnp.maximum(m[i], uk)
+                alpha = jnp.exp(m[i] - p)
+                beta = jnp.exp(uk - p)
+                yb[c, at, :] = (alpha * a[i] + beta * v) / (alpha * b[i] + beta)
+                m[i], a[i], b[i] = step_state(m[i], a[i], b[i], w_ref[:, lane(c)], k, v)
+
+
+def step_state(m, a, b, w, k, v):
+    mw = m - w
+    mn = jnp.maximum(mw, k)
+    keep = jnp.exp(mw - mn)
+    take = jnp.exp(k - mn)
+    return mn, keep * a + take * v, keep * b + take
+
+
+def interleave(work, step, first, total, last):
+    at = first
+    for i, piece in enumerate(work):
+        piece()
+        goal = first + (last - first) * (i + 1) // len(work)
+        while at < goal:
+            step(at)
+            at += 1
+    while at < total:
+        step(at)
+        at += 1
+
+
+def forward_body(nd, nz, seqs, pieces, lag, count, *refs):
+    ins, refs = refs[:count], refs[count:]
+    x_ref, n1g, n1b, mk, mv, mr, w_ref, u_ref, n2g, n2b, ck, cr, prev_a, prev_f = refs[:14]
+    outs, refs = refs[14:14 + count], refs[14 + count:]
+    first, before, gated, chan_key, chan_rec, r_ref, middle, diff2, kb, vb, yb, mb, ab, bb = refs[:14]
+    (key_in, value_in, recept_in, wbuf, sbuf, init, sm, sa, sb, halo, xs, xr, second,
+     loc, zs, zr, as_, ar, bs, br, ds, dr, hs, hr, es, er, ws) = refs[14:]
     d, z, y, x = place(nd, nz)
-    meet(partners(nd, nz, d, z, y, x))
+    rows, dim = x_ref.shape
+    part = dim // nd
+    chunks = rows // STEP
+    nt = 4 * nz
+    span = nt // seqs
+    t = lax.axis_index("tensor")
+    seq = t // span
+    pos = lax.rem(t, span)
+    f32 = jnp.float32
+
+    def mate(i):
+        return (d, seq * span + lax.rem(pos + i, span))
+
+    meet(partners(nd, nz, d, z, y, x) + [mate(i) for i in range(1, span)])
 
     def own(p):
         a, at, n = pieces[p]
@@ -317,30 +326,32 @@
     def first_pair(p, mine):
         a, at, n = pieces[p]
         if p % 2 == 0:
-            part = outs[a].at[d, :, y if mine else 1 - y, x, at:at + n]
+            block = outs[a].at[d, :, y if mine else 1 - y, x, at:at + n]
             to = spot(d, z, 1 - y, x)
         else:
-            part = outs[a].at[d, :, y, x if mine else 1 - x, at:at + n]
+            block = outs[a].at[d, :, y, x if mine else 1 - x, at:at + n]
             to = spot(d, z, y, 1 - x)
-        return send(part, part, as_.at[p], ar.at[p], to)
+        return send(block, block, as_.at[p], ar.at[p], to)
 
     def second_pair(p, mine):
         a, at, n = pieces[p]
         if p % 2 == 0:
-            part = outs[a].at[d, :, :, x if mine else 1 - x, at:at + n]
+            block = outs[a].at[d, :, :, x if mine else 1 - x, at:at + n]
             to = spot(d, z, y, 1 - x)
         else:
-            part = outs[a].at[d, :, y if mine else 1 - y, :, at:at + n]
+            block = outs[a].at[d, :, y if mine else 1 - y, :, at:at + n]
             to = spot(d, z, 1 - y, x)
-        return send(part, part, bs.at[p], br.at[p], to)
+        return send(block, block, bs.at[p], br.at[p], to)
 
     def along_d(p, i, source):
         a, at, n = pieces[p]
-        part = outs[a].at[source, :, :, :, at:at + n]
-        return send(part, part, ds.at[p, i - 1], dr.at[p, i - 1], spot(lax.rem(d + i, nd), z, y, x))
+        block = outs[a].at[source, :, :, :, at:at + n]
+        return send(block, block, ds.at[p, i - 1], dr.at[p, i - 1], spot(lax.rem(d + i, nd), z, y, x))
 
     total = len(pieces)
-    for step in range(total + 3 * lag):
+    arrived = set()
+
+    def gather_step(step):
         p = step
         if p < total:
             own(p).start()
@@ -361,9 +372,185 @@
             second_pair(p, False).wait_recv()
             for i in range(1, nd):
                 along_d(p, i, d).start()
+
+    def have(array):
+        for p in range(total):
+            if pieces[p][0] == array and p not in arrived:
+                arrived.add(p)
+                for i in range(1, nd):
+                    along_d(p, i, lax.rem(d - i + nd, nd)).wait_recv()
+
+    def fetch(array, slot):
+        return pltpu.make_async_copy(outs[array], wbuf.at[slot], ws.at[slot])
+
+    def norm_first():
+        @pl.loop(0, rows // 32)
+        def _(i):
+            at = pl.ds(pl.multiple_of(i * 32, 32), 32)
+            first[at, :] = (rowwise_norm(x_ref[at, :]) * n1g[...] + n1b[...]).astype(jnp.bfloat16)
+        pass_last(first, 0, 1).start()
+
+    def pass_last(rows_ref, slot, to):
+        return send(rows_ref.at[rows - 16:rows], halo.at[slot], hs.at[slot], hr.at[slot], mate(to))
+
+    def shifted(rows_ref, slot, prev, cols):
+        now = rows_ref[:, cols].astype(f32)
+        edge = jnp.where(pos == 0, prev[:, cols], halo[slot, :, cols].astype(f32)[15:16, :])
+        top = lax.broadcasted_iota(jnp.int32, now.shape, 0) == 0
+        return now, jnp.where(top, edge, pltpu.roll(now, 1, 0))
+
+    def mix_first():
+        pass_last(first, 0, 1).wait()
+
+        @pl.loop(0, dim // LANES)
+        def _(c):
+            cols = pl.ds(pl.multiple_of(c * LANES, LANES), LANES)
+            now, old = shifted(first, 0, prev_a, cols)
+            before[:, cols] = old.astype(jnp.bfloat16)
+            for mix, dst in ((mk, key_in), (mv, value_in), (mr, recept_in)):
+                dst[:, cols] = (now * mix[:, cols] + old * (1.0 - mix[:, cols])).astype(jnp.bfloat16)
+
+    def project(array, slot, left, store):
+        def run():
+            fetch(array, slot).wait()
+            wide = min(256, dim)
+            per = 4 * nz * pieces_rows[array] // (dim // wide)
+            weights = wbuf.at[slot].reshape(nd, dim, part)
+            for n in range(dim // wide):
+                acc = dot_nt(left[:, :part], weights[0, n * wide:(n + 1) * wide])
+                for e in range(1, nd):
+                    acc = acc + dot_nt(left[:, e * part:(e + 1) * part], weights[e, n * wide:(n + 1) * wide])
+                store(n, wide, acc)
+        return run
+
+    pieces_rows = [s.shape[0] for s in ins]
+
+    def into_blocks(dst):
+        def store(n, wide, acc):
+            for q in range(wide // LANES):
+                dst[n * (wide // LANES) + q] = acc[:, lane(q)]
+        return store
+
+    def into_rows(n, wide, acc):
+        r_ref[:, n * wide:(n + 1) * wide] = acc
+
+    def get_kv():
+        have(1)
+        fetch(1, 0).start()
+        have(2)
+        fetch(2, 1).start()
+
+    def get_r():
+        have(3)
+        fetch(3, 0).start()
+        have(0)
+        copy = pltpu.make_async_copy(outs[0].at[d], sbuf, ws.at[2])
+        copy.start()
+        copy.wait()
+        head = dim // nt
+        per = LANES // head
+        for c in range(dim // LANES):
+            cells = []
+            for q in range(per):
+                b = c * per + q
+                cells.append(sbuf[b // 4, (b // 2) % 2, b % 2][:, :head])
+            init[:, lane(c)] = jnp.concatenate(cells, axis=1)
+
+    def get_o():
+        have(4)
+        fetch(4, 1).start()
+
+    def initial(j):
+        got = init[j:j + 1, :]
+        for s in range(1, seqs):
+            got = jnp.where(seq == s, init[3 * s + j:3 * s + j + 1, :], got)
+        return got
+
+    def share(i):
+        return send(xs, xr.at[i - 1], es.at[i - 1], er.at[i - 1], mate(i))
+
+    def summarize():
+        scan_ends(kb, vb, w_ref, sm, sa, sb, dim, chunks)
+        lead = pos == 0
+        m = jnp.where(lead, initial(2), NEG)
+        a = jnp.where(lead, initial(0), 0.0)
+        b = jnp.where(lead, initial(1), 0.0)
+        decay = float(STEP) * w_ref[...]
+        for s in range(chunks):
+            m, a, b = join(m, a, b, decay, sm[s:s + 1, :], sa[s:s + 1, :], sb[s:s + 1, :])
+        xs[0:1, :] = a
+        xs[1:2, :] = b
+        xs[2:3, :] = m
+        xs[3:8, :] = jnp.zeros((5, dim), f32)
+        for i in range(1, span):
+            share(i).start()
+
+    def carry_in():
+        for i in range(1, span):
+            share(i).wait()
+        m = jnp.where(pos == 0, initial(2), NEG)
+        a = jnp.where(pos == 0, initial(0), 0.0)
+        b = jnp.where(pos == 0, initial(1), 0.0)
+        decay = float(rows) * w_ref[...]
+        for i in range(span - 1, 0, -1):
+            on = i <= pos
+            mn, an, bn = join(m, a, b, decay, xr[i - 1, 2:3, :], xr[i - 1, 0:1, :], xr[i - 1, 1:2, :])
+            m, a, b = jnp.where(on, mn, m), jnp.where(on, an, a), jnp.where(on, bn, b)
+        decay = float(STEP) * w_ref[...]
+        for s in range(chunks):
+            me, ae, be = sm[s:s + 1, :], sa[s:s + 1, :], sb[s:s + 1, :]
+            sm[s:s + 1, :] = m
+            sa[s:s + 1, :] = a
+            sb[s:s + 1, :] = b
+            m, a, b = join(m, a, b, decay, me, ae, be)
+
+    def scan():
+        scan_rows(kb, vb, yb, mb, ab, bb, w_ref, u_ref, sm, sa, sb, dim, chunks)
+        for c in range(dim // LANES):
+            gated[:, lane(c)] = (jax.nn.sigmoid(r_ref[:, lane(c)]) * yb[c]).astype(jnp.bfloat16)
+
+    def attend_out():
+        fetch(4, 1).wait()
+        weights = wbuf.at[1].reshape(nd, dim, part)
+        wide = min(256, part)
+        for e in range(nd):
+            for n in range(part // wide):
+                at = slice(e * part + n * wide, e * part + (n + 1) * wide)
+                middle[:, at] = x_ref[:, at] + dot_nn(gated[...], weights[e, :, n * wide:(n + 1) * wide])
+
+    def norm_second():
+        @pl.loop(0, rows // 32)
+        def _(i):
+            at = pl.ds(pl.multiple_of(i * 32, 32), 32)
+            second[at, :] = (rowwise_norm(middle[at, :]) * n2g[...] + n2b[...]).astype(jnp.bfloat16)
+        pass_last(second, 1, 1).start()
+
+    def mix_second():
+        pass_last(second, 1, 1).wait()
+
+        @pl.loop(0, dim // LANES)
+        def _(c):
+            cols = pl.ds(pl.multiple_of(c * LANES, LANES), LANES)
+            now, old = shifted(second, 1, prev_f, cols)
+            diff2[:, cols] = now - old
+            for mix, dst in ((ck, chan_key), (cr, chan_rec)):
+                dst[:, cols] = (now * mix[:, cols] + old * (1.0 - mix[:, cols])).astype(jnp.bfloat16)
+
+    steps = total + 3 * lag
+    gather_step(0)
+    gather_step(1)
+    norm_first()
+    gather_step(2)
+    mix_first()
+    ready = 1 + max(p for p in range(total) if pieces[p][0] <= 4) + 3 * lag
+    for s in range(3, ready):
+        gather_step(s)
+    work = [get_kv, project(1, 0, key_in, into_blocks(kb)), project(2, 1, value_in, into_blocks(vb)), get_r, get_o, summarize,
+            project(3, 0, recept_in, into_rows), carry_in, scan, attend_out, norm_second, mix_second]
+    interleave(work, gather_step, ready, steps, min(steps, ready + 10))
+    for a in range(count):
+        have(a)
     for p in range(total):
-        for i in range(1, nd):
-            along_d(p, i, lax.rem(d - i + nd, nd)).wait_recv()
         for i in range(1, nz):
             along_z(p, i, z).wait_send()
         first_pair(p, True).wait_send()
@@ -372,24 +559,39 @@
             along_d(p, i, d).wait_send()
 
 
-def gather_weights(nd, nt, shards, unit, lag=1, space=None):
+def forward_block(nd, nt, shards, vectors, seqs, rows, unit, lag):
     nz = nt // 4
+    span = nt // seqs
+    dim = shards[1].shape[0] * nt
+    part = dim // nd
     pieces = []
     for a, s in enumerate(shards):
         pieces += [(a, at, min(unit, s.shape[0])) for at in range(0, s.shape[0], unit)]
     n = len(pieces)
     dma = pltpu.SemaphoreType.DMA
-    outs = pl.pallas_call(
-        functools.partial(gather_body, nd, nz, pieces, lag, len(shards)),
-        out_shape=tuple(jax.ShapeDtypeStruct((nd, nz, 2, 2) + s.shape, s.dtype) for s in shards),
-        in_specs=[HBM] * len(shards),
-        out_specs=[space or HBM] * len(shards),
-        scratch_shapes=[dma((n,)), dma((n, nz - 1)), dma((n, nz - 1)), dma((n,)), dma((n,)), dma((n,)), dma((n,)),
-                        dma((n, nd - 1)), dma((n, nd - 1))],
+    bf, f32 = jnp.bfloat16, jnp.float32
+    low = jax.ShapeDtypeStruct((rows, dim), bf)
+    full = jax.ShapeDtypeStruct((rows, dim), f32)
+    block = jax.ShapeDtypeStruct((dim // LANES, rows, LANES), f32)
+    chunks = rows // STEP
+    per = shards[1].shape[0]
+    got = pl.pallas_call(
+        functools.partial(forward_body, nd, nz, seqs, pieces, lag, len(shards)),
+        out_shape=tuple(jax.ShapeDtypeStruct((nd, nz, 2, 2) + s.shape, s.dtype) for s in shards)
+        + (low,) * 5 + (full,) * 3 + (block,) * 6,
+        in_specs=[HBM] * len(shards) + [VMEM] * len(vectors),
+        out_specs=[HBM] * len(shards) + [VMEM] * 14,
+        scratch_shapes=[pltpu.VMEM((rows, dim), bf)] * 3
+        + [pltpu.VMEM((2, nd, nz, 2, 2, per, part), bf), pltpu.VMEM((nz, 2, 2) + shards[0].shape, f32), pltpu.VMEM((shards[0].shape[0], dim), f32)]
+        + [pltpu.VMEM((chunks, dim), f32)] * 3
+        + [pltpu.VMEM((2, 16, dim), bf), pltpu.VMEM((8, dim), f32), pltpu.VMEM((span - 1, 8, dim), f32), pltpu.VMEM((rows, dim), bf)]
+        + [dma((n,)), dma((n, nz - 1)), dma((n, nz - 1)), dma((n,)), dma((n,)), dma((n,)), dma((n,)),
+           dma((n, nd - 1)), dma((n, nd - 1)), dma((2,)), dma((2,)), dma((span - 1,)), dma((span - 1,)), dma((3,))],
         compiler_params=pltpu.CompilerParams(collective_id=0, has_side_effects=True, vmem_limit_bytes=58 * 2**20),
-        name="gather_weights",
-    )(*shards)
-    return [o.reshape(nd, nt * s.shape[0], s.shape[1]) for o, s in zip(outs, shards)]
+        name="forward_block",
+    )(*shards, *vectors)
+    weights = [o.reshape(nd, nt * s.shape[0], s.shape[1]) for o, s in zip(got[1:len(shards)], shards[1:])]
+    return weights, got[len(shards):]
 
 
 def add_tiles(dst, src, tiles):
@@ -407,12 +609,12 @@
 
     def load(c):
         a, at = chunks[c]
-        return pltpu.make_async_copy(grads[a].at[d, :, :, :, at:at + rc], own.at[c], loc.at[c])
+        return pltpu.make_async_copy(grads[a].at[:, :, :, at:at + rc, pl.ds(pl.multiple_of(d * part, part), part)], own.at[c], loc.at[c])
 
     def along_d(c, i):
         a, at = chunks[c]
         to = lax.rem(d + i, nd)
-        return send(grads[a].at[to, :, :, :, at:at + rc], sib.at[i - 1, c], ds.at[i - 1, c], dr.at[i - 1, c], spot(to, z, y, x))
+        return send(grads[a].at[:, :, :, at:at + rc, pl.ds(pl.multiple_of(to * part, part), part)], sib.at[i - 1, c], ds.at[i - 1, c], dr.at[i - 1, c], spot(to, z, y, x))
 
     def first_pair(c):
         if c % 2 == 0:
@@ -540,11 +742,11 @@
 
 def scatter_grads(nd, nt, grads, vec, top, rc, lag=2, ahead=3):
     nz = nt // 4
-    part = grads[0].shape[2]
-    split = [g.reshape(nd, nz, 2, 2, g.shape[1] // nt, part) for g in grads]
+    part = grads[0].shape[1] // nd
+    split = [g.reshape(nz, 2, 2, g.shape[0] // nt, g.shape[1]) for g in grads]
     chunks = []
     for a, g in enumerate(split):
-        chunks += [(a, at) for at in range(0, g.shape[4], rc)]
+        chunks += [(a, at) for at in range(0, g.shape[3], rc)]
     n = len(chunks)
     dma = pltpu.SemaphoreType.DMA
     bf = jnp.bfloat16
@@ -579,12 +781,7 @@
     pos = tp % span
     part = dim // nd
     head = num.shape[1]
-    ahead = [(i, i + 1) for i in range(nt - 1)]
     behind = [(i + 1, i) for i in range(nt - 1)]
-
-    whole_k, whole_v, whole_r, whole_o, whole_fk, whole_fv, whole_fr = gather_weights(
-        nd, nt, [s.T for s in (wk, wv, wr, wo, fk, fv, fr)], 32, 2)
-    states = lax.all_gather(jnp.stack([num, den, top]), "tensor", axis=2, tiled=True)
 
     def into(left, whole):
         total = dot_nt(left[:, :part], whole[0])
@@ -596,53 +793,31 @@
         return jnp.concatenate([dot_nn(left, whole[d]) for d in range(nd)], axis=1)
 
     def weight_grad(cols, ins):
-        both = dot_tn(cols, ins).astype(jnp.bfloat16)
-        return jnp.stack([both[:, d * part:(d + 1) * part] for d in range(nd)])
-
-    def prior(rows_now, previous):
-        halo = lax.ppermute(rows_now[-1:, :], "tensor", ahead)
-        mine = lax.dynamic_slice_in_dim(previous, seq, 1, 0)
-        first = jnp.where(pos == 0, mine, halo)
-        return jnp.concatenate([first, rows_now[:-1, :]], axis=0)
+        return dot_tn(cols, ins).astype(jnp.bfloat16)
 
     def pushed(back):
         halo = lax.ppermute(back[:1, :], "tensor", behind)
         last = jnp.where(pos == span - 1, 0.0, halo)
         return jnp.concatenate([back[1:, :], last], axis=0)
 
+    def line(v):
+        return v.astype(jnp.float32).reshape(1, dim)
+
+    w = jnp.exp(fading)
+    packed = jnp.stack([num, den, top], axis=1).reshape(3 * seqs, head)
+    packed = jnp.pad(packed, ((0, -3 * seqs % 8), (0, LANES - head)))
+    shards = [packed] + [s.T for s in (wk, wv, wr, wo, fr, fk, fv)]
+    mine_a = lax.dynamic_slice_in_dim(prev_a, seq, 1, 0)
+    mine_f = lax.dynamic_slice_in_dim(prev_f, seq, 1, 0)
+    vectors = [x] + [line(v) for v in (n1g, n1b, mk, mv, mr, w, reward, n2g, n2b, ck, cr, mine_a, mine_f)]
+    weights, saved = forward_block(nd, nt, shards, vectors, seqs, rows, 32, 2)
+    whole_k, whole_v, whole_r, whole_o, whole_fr, whole_fk, whole_fv = weights
+    first, before, gated, chan_key, chan_rec, recept, middle, diff2, kb, vb, yb, mb, ab, bb = saved
+    wr_, ur_ = w[None, :], reward[None, :]
     s1, scale1 = norm_stats(x)
-    first = (s1 * n1g + n1b).astype(jnp.bfloat16)
-    before = prior(first, prev_a)
+    s2, scale2 = norm_stats(middle)
     key_in, value_in, recept_in = blended(first, before, mk), blended(first, before, mv), blended(first, before, mr)
-    keys, vals, recept = into(key_in, whole_k), into(value_in, whole_v), into(recept_in, whole_r)
-
-    w = jnp.exp(fading)
-    steps = jnp.arange(rows, dtype=jnp.float32)[:, None]
-    tail = keys - (rows - 1.0 - steps) * w
-    m_loc = jnp.max(tail, axis=0)
-    e_loc = jnp.exp(tail - m_loc)
-    sent = jnp.stack([jnp.sum(e_loc * vals, axis=0), jnp.sum(e_loc, axis=0), m_loc])
-    got = lax.all_gather(sent, "tensor", axis=0)
-    mine = lax.dynamic_slice_in_dim(got, seq * span, span, 0)
-    start = lax.dynamic_index_in_dim(states, seq, 1, keepdims=False)
-    a, b, m = start[0], start[1], start[2]
-    for i in range(span - 1):
-        on = i < pos
-        mw = m - rows * w
-        mn = jnp.maximum(mw, mine[i, 2])
-        keep, take = jnp.exp(mw - mn), jnp.exp(mine[i, 2] - mn)
-        a = jnp.where(on, keep * a + take * mine[i, 0], a)
-        b = jnp.where(on, keep * b + take * mine[i, 1], b)
-        m = jnp.where(on, mn, m)
-    wr_, ur_ = w[None, :], reward[None, :]
-    gated, kb, vb, yb, mb, ab, bb = wkv_forward(keys, vals, recept, wr_, ur_, a[None, :], b[None, :], m[None, :])
-    middle = x + outof(gated, whole_o)
-
-    s2, scale2 = norm_stats(middle)
-    second = (s2 * n2g + n2b).astype(jnp.bfloat16)
-    before2 = prior(second, prev_f)
-    chan_key = blended(second, before2, ck)
-    chan_rec = blended(second, before2, cr)
+
     hidden = jnp.maximum(into(chan_key, whole_fk), 0.0)
     squared = jnp.square(hidden).astype(jnp.bfloat16)
     chan_values = outof(squared, whole_fv)
@@ -658,7 +833,6 @@
     g_hidden = (g_squared * 2.0 * hidden).astype(jnp.bfloat16)
     grad_fk = weight_grad(g_hidden, chan_key)
     g_key_in = outof(g_hidden, whole_fk)
-    diff2 = second.astype(jnp.float32) - before2.astype(jnp.float32)
     grad_ck = jnp.sum(g_key_in * diff2, axis=0)
     grad_cr = jnp.sum(g_rec_in * diff2, axis=0)
     back2 = g_key_in * (1.0 - ck) + g_rec_in * (1.0 - cr)

time: 567 us -> 441 us (0.78)
  blocking collectives: 126 us -> 41.9 us
  other arithmetic: 42.9 us -> 12.7 us
  local copies, waits for them, and re-layouts: 67.6 us -> 49.5 us
  starting transfers between devices: 11.3 us -> 3.11 us
  Pallas kernels: 274 us -> 282 us
    all_gather x1 -> x0, blocking collectives: 48.2 us -> none  [local(): lax.all_gather(jnp.stack([num, den, top]), 'tensor', axis=2, tiled=True)]
    all_gather x2 -> x1, blocking collectives: 77.5 us -> 41.9 us  [local(): got = lax.all_gather(sent, 'tensor', axis=0)]
    another operation x8 -> x1, other arithmetic: 24.4 us -> 0.72 us  [local(): packed = jnp.stack([num, den, top], axis=1).reshape(3 * seqs, head)]
    slice x11 -> x0, local copies, waits for them, and re-layouts: 22.8 us -> none  [the longest x7 11.7 us: weight_grad(): return jnp.stack([both[:, d * part:(d + 1) * part] for d in range(nd)])]
    dot_general x7, matrix products: 12 us -> 23.3 us  [dot_tn(): lax.dot_general(x, y, (((0,), (0,)), ((), ())), preferred_element_type=jn...]
    unnamed x190 -> x150, local copies, waits for them, and re-layouts: 12.9 us -> 22.6 us
    ppermute x2 -> x0, starting transfers between devices: 8.69 us -> none  [prior(): halo = lax.ppermute(rows_now[-1:, :], 'tensor', ahead)]
    pallas_call x2 -> x1, Pallas kernels: 134 us -> 142 us  [forward_block(): pl.pallas_call(functools.partial(forward_body, nd, nz, seqs, pieces, lag,...]
  transfers between devices with their start and end apart: 4 -> 2, of which waited for: 1 -> 0; matrix products, arithmetic and copies ran while one was open for 13% -> 6% of each run, Pallas kernels for 23% -> 0%
where the time goes in v3:
time: 441 us; the launch traced here: 433 us
  Pallas kernels  282 us (64%)
  local copies, waits for them, and re-layouts  49.5 us (11%)
  matrix products  41.9 us (10%)
  blocking collectives  41.9 us (10%)
  other arithmetic  12.7 us (3%)
    pallas_call x1, Pallas kernels, forward_block(): pl.pallas_call(functools.partial(forward_body, nd, nz, seqs, pieces, lag,...  142 us
    pallas_call x1, Pallas kernels, scatter_grads(): pl.pallas_call(functools.partial(scatter_body, nd, nz, chunks, rc, part,...  133 us
    all_gather x1, blocking collectives, local(): got = lax.all_gather(sent, 'tensor', axis=0)  41.9 us
    dot_general x7, matrix products, dot_tn(): lax.dot_general(x, y, (((0,), (0,)), ((), ())), preferred_element_type=jn...  23.3 us
    unnamed x150, local copies, waits for them, and re-layouts  22.6 us
    dot_general x12, matrix products, dot_nn(): lax.dot_general(x, y, (((1,), (0,)), ((), ())), preferred_element_type=jn...  10.2 us
  transfers between devices with their start and end apart: 2, of which 0 were waited for; matrix products, arithmetic and copies ran while one was open for 6% of the time, Pallas kernels for 0%

profile of v3, /device:TPU:0, one launch (start us, length us, event | category | flops | bytes accessed | tf_op | source)
XLA Modules:
  0.0 433.3 jit_solution(7517548164555085589)
XLA Ops:
  1.4 1.8 copy.61
  3.2 1.8 copy.62
  5.0 1.3 exp.404
  6.9 1.3 fusion.37
  8.2 141.9 %forward_block.1 = (f32[2,4,2,2,8,128]{5,4,3,2,1,0:T(8,128)}, bf16[2,4,2,2,64,512]{5,4,3,2,1,0:T(8,128)(2,1)}, bf16[2,4,2,2,64,512]{5,4,3,2,1,0:T(8,128)(2,1)}, ...) custom-call(f32[8,128]{1,0:T(8,128)} %pad.4.refs_0_, ...), custom_call_target="tpu_custom_call" | custom-call | tf_op jit(solution)/shard_map/forward_block/pallas_call | solution.py:578
  150.1 4.0 fusion.137
  154.1 3.8 copy-done.25
  159.1 1.3 fusion.30
  161.0 1.3 copy-done.17
  162.3 1.3 fusion.1
  163.7 2.2 fusion.134
  165.8 2.0 fusion.135
  169.7 1.9 multiply_convert_fusion.2
  172.5 2.0 copy-done.15
  174.5 1.3 fusion.27
  176.7 1.3 copy-done.13
  178.0 1.3 fusion.3
  180.2 1.3 fusion.147
  182.4 1.3 fusion.146
  185.2 1.8 collective-permute-start
  187.2 6.9 %convolution_convert_fusion.1 = bf16[4096,1024]{1,0:T(8,128)(2,1)} fusion(bf16[256,4096]{1,0:T(8,128)(2,1)S(1)} %fusion.3, bf16[256,1024]{1,0:T(8,128)(2,1)} %get-tuple-element.63), kind=kOutput, calls=%fused_computation.1 | convolution fusion | flops 2151677952 | bytes 11010048 | tf_op jit(solution)/shard_map/dot_general | solution.py:40
  194.1 5.7 %convolution_convert_fusion = bf16[4096,1024]{1,0:T(8,128)(2,1)} fusion(bf16[256,1024]{1,0:T(8,128)(2,1)S(1)} %copy-done.47, f32[256,4096]{1,0:T(8,128)S(1)} %copy-done.11), kind=kOutput, calls=%fused_computation | convolution fusion | flops 2153775104 | bytes 13107200 | tf_op jit(solution)/shard_map/dot_general | solution.py:40
  199.8 2.1 convolution_convert_fusion.2
  202.2 1.6 fusion.142
  203.8 1.6 fusion.141
  205.4 1.6 fusion.140
  207.1 1.6 fusion.139
  208.6 2.3 slice.501
  211.0 2.3 multiply_reduce_fusion.2
  213.5 1.4 fusion.136
  216.6 2.5 wkv_carry.1
  219.1 41.9 %all-gather.1 = f32[16,3,1024]{2,1,0:T(4,128)S(1)} all-gather(f32[1,3,1024]{2,1,0:T(4,128)S(1)} %maximum_bitcast_fusion), channel_id=2, replica_groups=mesh['dp'=2,'tensor'=16] {'tensor'}, dimensions={0}, use_global_device_ids=true | all-gather | bytes 208896 | tf_op jit(solution)/shard_map/all_gather | solution.py:848
  261.2 5.0 %wkv_backward.1 = (bf16[256,1024]{1,0:T(8,128)(2,1)S(1)}, bf16[256,1024]{1,0:T(8,128)(2,1)S(1)}, bf16[256,1024]{1,0:T(8,128)(2,1)S(1)}, f32[1,1024]{1,0:T(1,128)S(1)}, f32[1,1024]{1,0:T(1,128)S(1)}) custom-call(f32[256,1024]{1,0:T(8,128)S(1)} %copy-done, f32[256,1024]{1,0:T(8,128)S(1)} %convolution_add_fusion.2.gg_ref, f32[8,256,128]{2,1,0:T(8,128)S(1)} %copy-done.1, ...), custom_call_target="tpu_custom_call" | custom-call | flops 20971520 | bytes 11534336 | tf_op jit(solution)/shard_map/wkv_backward/pallas_call | solution.py:175
  269.2 2.2 convolution_convert_fusion.6
  271.4 2.2 convolution_convert_fusion.5
  273.5 2.2 convolution_convert_fusion.4
  276.3 1.3 collective-permute-start.1
  277.6 2.1 convolution_convert_fusion.3
  282.0 3.2 multiply_reduce_fusion.6
  285.2 1.9 concatenate.46.refs_7_
  287.1 132.8 %scatter_grads.1 = (f32[832,512]{1,0:T(8,128)}, f32[24,1024]{1,0:T(8,128)}) custom-call(bf16[4,2,2,64,1024]{4,3,2,1,0:T(8,128)(2,1)} %bitcast.325, bf16[4,2,2,64,1024]{4,3,2,1,0:T(8,128)(2,1)} %bitcast.326, bf16[4,2,2,64,1024]{4,3,2,1,0:T(8,128)(2,1)} %bitcast.327, bf16[4,2,2,64,1024]{4,3,2,1,0:T(8,128)(2,1)} %bitcast.329, ...), custom_call_target="tpu_custom_call" | custom-call | tf_op jit(solution)/shard_map/scatter_grads/pallas_call | solution.py:758
  420.0 1.5 fusion.145
  421.5 1.9 fusion.144
  423.4 2.0 slice_bitcast_fusion.2
  425.4 2.2 slice_bitcast_fusion
  427.6 2.0 copy.63
  429.7 2.0 copy.64
  431.7 1.3 multiply_add_fusion
  (194 shorter events, 17.8 us)
Async XLA Ops:
  150.1 7.8 %copy-start.25 = (bf16[2,4,2,2,256,512]{5,4,3,2,1,0:T(8,128)(2,1)S(1)}, bf16[2,4,2,2,256,512]{5,4,3,2,1,0:T(8,128)(2,1)}, u32[]{:S(2)}) copy-start(bf16[2,4,2,2,256,512]{5,4,3,2,1,0:T(8,128)(2,1)} %get-tuple-element.64) | copy-start | bytes 25165828
  154.1 9.6 %copy-start.12 = (bf16[1,4,2,2,256,512]{5,4,3,2,1,0:T(8,128)(2,1)}, bf16[1,4,2,2,256,512]{5,4,3,2,1,0:T(8,128)(2,1)S(1)}, u32[]{:S(2)}) copy-start(bf16[1,4,2,2,256,512]{5,4,3,2,1,0:T(8,128)(2,1)S(1)} %get-tuple-element.193) | copy-start | bytes 12582916
  154.1 11.7 %copy-start.14 = (bf16[1,4,2,2,256,512]{5,4,3,2,1,0:T(8,128)(2,1)}, bf16[1,4,2,2,256,512]{5,4,3,2,1,0:T(8,128)(2,1)S(1)}, u32[]{:S(2)}) copy-start(bf16[1,4,2,2,256,512]{5,4,3,2,1,0:T(8,128)(2,1)S(1)} %get-tuple-element.192) | copy-start | bytes 12582916
  159.0 3.3 copy-start.17
  171.6 4.2 copy-start.46
  171.6 2.9 copy-start.15
  172.0 11.8 %copy-start.28 = (f32[256,512]{1,0:T(8,128)}, f32[256,512]{1,0:T(8,128)S(1)}, u32[]{:S(2)}) copy-start(f32[256,512]{1,0:T(8,128)S(1)} %fusion.149) | copy-start | bytes 1572868
  172.5 11.3 %copy-start.30 = (f32[256,512]{1,0:T(8,128)}, f32[256,512]{1,0:T(8,128)S(1)}, u32[]{:S(2)}) copy-start(f32[256,512]{1,0:T(8,128)S(1)} %fusion.148) | copy-start | bytes 1572868
  174.5 3.5 copy-start.13
  182.4 4.6 %copy-start.16 = (f32[256,1024]{1,0:T(8,128)S(1)}, f32[256,1024]{1,0:T(8,128)}, u32[]{:S(2)}) copy-start(f32[256,1024]{1,0:T(8,128)} %refs_8_.1) | copy-start | bytes 3145732
  183.7 3.4 copy-start.64
  183.7 3.4 copy-start.65
  183.7 3.4 copy-start.63
  185.2 25.8 %collective-permute-start = (f32[1,1024]{1,0:T(1,128)S(1)}, f32[1,1024]{1,0:T(1,128)S(1)}, u32[]{:S(2)}, u32[]{:S(2)}) collective-permute-start(f32[1,1024]{1,0:T(1,128)S(1)} %get-tuple-element.222), channel_id=1, source_target_pairs={{1,0},{2,1},{3,2},{4,3},{5,4},{6,5},{7,6},{8,7},{9,8},{10,9},{11,1... | collective-permute-start | bytes 12296 | tf_op jit(solution)/shard_map/ppermute | solution.py:799
  187.2 6.9 %copy-start.11 = (f32[256,4096]{1,0:T(8,128)S(1)}, f32[256,4096]{1,0:T(8,128)}, u32[]{:S(2)}) copy-start(f32[256,4096]{1,0:T(8,128)} %copy-done.9) | copy-start | bytes 12582916
  187.2 6.9 %copy-start.47 = (bf16[256,1024]{1,0:T(8,128)(2,1)S(1)}, bf16[256,1024]{1,0:T(8,128)(2,1)}, u32[]{:S(2)}) copy-start(bf16[256,1024]{1,0:T(8,128)(2,1)} %copy-done.46) | copy-start | bytes 1572868
  194.1 5.7 %copy-start.33 = (bf16[256,1024]{1,0:T(8,128)(2,1)S(1)}, bf16[256,1024]{1,0:T(8,128)(2,1)}, u32[]{:S(2)}) copy-start(bf16[256,1024]{1,0:T(8,128)(2,1)} %copy-done.32) | copy-start | bytes 1572868
  194.1 5.7 %copy-start.56 = (bf16[256,1024]{1,0:T(8,128)(2,1)S(1)}, bf16[256,1024]{1,0:T(8,128)(2,1)}, u32[]{:S(2)}) copy-start(bf16[256,1024]{1,0:T(8,128)(2,1)} %get-tuple-element.61) | copy-start | bytes 1572868
  199.8 4.0 copy-start.50
  202.2 3.3 copy-start.49
  203.8 3.2 copy-start.48
  207.0 4.0 copy-start.22
  207.0 4.0 copy-start.29
  207.0 4.0 copy-start.31
  207.0 4.0 copy-start.66
  211.0 2.4 copy-start.58
  211.0 3.8 copy-start.42
  213.4 2.4 copy-start
  213.4 2.4 copy-start.1
  213.4 2.5 copy-start.2
  213.4 2.8 copy-start.3
  213.4 3.1 copy-start.4
  213.5 3.1 copy-start.7
  213.5 3.1 copy-start.8
  215.8 45.3 %copy-start.5 = (f32[8,256,128]{2,1,0:T(8,128)S(1)}, f32[8,256,128]{2,1,0:T(8,128)}, u32[]{:S(2)}) copy-start(f32[8,256,128]{2,1,0:T(8,128)} %get-tuple-element.69.vb) | copy-start | bytes 3145732
  215.8 45.3 %copy-start.6 = (f32[8,256,128]{2,1,0:T(8,128)S(1)}, f32[8,256,128]{2,1,0:T(8,128)}, u32[]{:S(2)}) copy-start(f32[8,256,128]{2,1,0:T(8,128)} %get-tuple-element.72.ab) | copy-start | bytes 3145732
  261.2 5.0 %copy-start.40 = (bf16[1,4,2,2,64,512]{5,4,3,2,1,0:T(8,128)(2,1)S(1)}, bf16[1,4,2,2,64,512]{5,4,3,2,1,0:T(8,128)(2,1)}, u32[]{:S(2)}) copy-start(bf16[1,4,2,2,64,512]{5,4,3,2,1,0:T(8,128)(2,1)} %get-tuple-element.203) | copy-start | bytes 3145732
  261.2 5.5 %copy-start.38 = (bf16[1,4,2,2,64,512]{5,4,3,2,1,0:T(8,128)(2,1)S(1)}, bf16[1,4,2,2,64,512]{5,4,3,2,1,0:T(8,128)(2,1)}, u32[]{:S(2)}) copy-start(bf16[1,4,2,2,64,512]{5,4,3,2,1,0:T(8,128)(2,1)} %get-tuple-element.202) | copy-start | bytes 3145732
  268.7 7.0 %copy-start.26 = (f32[256,512]{1,0:T(8,128)}, f32[256,512]{1,0:T(8,128)S(1)}, u32[]{:S(2)}) copy-start(f32[256,512]{1,0:T(8,128)S(1)} %fusion.151) | copy-start | bytes 1572868
  269.2 6.6 %copy-start.27 = (f32[256,512]{1,0:T(8,128)}, f32[256,512]{1,0:T(8,128)S(1)}, u32[]{:S(2)}) copy-start(f32[256,512]{1,0:T(8,128)S(1)} %fusion.150) | copy-start | bytes 1572868
  273.5 4.1 copy-start.62
  275.7 4.0 copy-start.70
  275.7 4.3 copy-start.71
  275.7 4.3 copy-start.72
  275.8 6.3 %copy-start.67 = (f32[1024]{0:T(1024)S(1)}, f32[1024]{0:T(1024)}, u32[]{:S(2)}) copy-start(f32[1024]{0:T(1024)} %param.31) | copy-start | bytes 12292
  276.3 5.7 %collective-permute-start.1 = (f32[1,1024]{1,0:T(1,128)S(1)}, f32[1,1024]{1,0:T(1,128)S(1)}, u32[]{:S(2)}, u32[]{:S(2)}) collective-permute-start(f32[1,1024]{1,0:T(1,128)S(1)} %get-tuple-element.220), channel_id=1, source_target_pairs={{1,0},{2,1},{3,2},{4,3},{5,4},{6,5},{7,6},{8,7},{9,8},{10,9},{11,1... | collective-permute-start | bytes 12296 | tf_op jit(solution)/shard_map/ppermute | solution.py:799
  420.0 11.7 %copy-start.43 = (f32[256,1024]{1,0:T(8,128)S(1)}, f32[256,1024]{1,0:T(8,128)}, u32[]{:S(2)}) copy-start(f32[256,1024]{1,0:T(8,128)} %get-tuple-element.190) | copy-start | bytes 3145732
  420.0 11.7 %copy-start.44 = (f32[256,1024]{1,0:T(8,128)S(1)}, f32[256,1024]{1,0:T(8,128)}, u32[]{:S(2)}) copy-start(f32[256,1024]{1,0:T(8,128)} %get-tuple-element.188) | copy-start | bytes 3145732
  (27 other events, 46.1 us)
